TPU v7x, 32 devices: a whole 2x2x4 slice. The times are simulated.
32 devices in a mesh: dp: 8 (over z, x), tensor: 4 (over y, core).
Axes of the slice: x: 2, y: 2, z: 4, core: 2. Of those that a mesh axis runs over, the one named last changes fastest.
Arguments:
- hidden_in: bfloat16 [16384, 768], P('dp'), may hold values from -6 to 6
- doc_ids: int32 [16384], P('dp'), may hold values from 0 to 7, as said below
- ln1_gain: float32 [768], replicated, may hold values from 0.5 to 1.5
- ln1_bias: float32 [768], replicated, may hold values from -1.25 to 1.25
- w_qkv: bfloat16 [768, 3, 12, 64], P(None, None, 'tensor'), may hold values from -0.3125 to 0.3125
- b_qv: float32 [2, 12, 64], P(None, 'tensor'), may hold values from -1.75 to 1.75
- w_out: bfloat16 [12, 64, 768], P('tensor'), may hold values from -0.875 to 0.875
- b_out: float32 [768], replicated, may hold values from -1.25 to 1.25
- ln2_gain: float32 [768], replicated, may hold values from 0.5 to 1.5
- ln2_bias: float32 [768], replicated, may hold values from -1.25 to 1.25
- w_fc: bfloat16 [768, 3072], P(None, 'tensor'), may hold values from -0.21875 to 0.21875
- b_fc: float32 [24, 128], P('tensor'), may hold values from -1.75 to 1.75
- w_proj: bfloat16 [3072, 768], P('tensor'), may hold values from -0.109375 to 0.109375
- b_proj: float32 [768], replicated, may hold values from -1.25 to 1.25
- grad_out: bfloat16 [16384, 768], P('dp'), may hold values from -6 to 6
Outputs:
- block_out: bfloat16 [16384, 768], P('dp')
- grad_in: float32 [16384, 768], P('dp')
- grad_ln1_gain: float32 [768], P('dp')
- grad_ln1_bias: float32 [768], P('dp')
- grad_w_qkv: float32 [768, 3, 12, 64], P('dp', None, 'tensor')
- grad_b_qv: float32 [2, 12, 64], P(None, 'tensor', 'dp')
- grad_w_out: float32 [12, 64, 768], P('tensor', None, 'dp')
- grad_b_out: float32 [768], P('dp')
- grad_ln2_gain: float32 [768], P('dp')
- grad_ln2_bias: float32 [768], P('dp')
- grad_w_fc: float32 [768, 3072], P('dp', 'tensor')
- grad_b_fc: float32 [24, 128], P('tensor', 'dp')
- grad_w_proj: float32 [3072, 768], P('tensor', 'dp')
- grad_b_proj: float32 [768], P('dp')
Inputs may be any that keep to these rules, and one draw needn't show every extreme that they name: `doc_ids`: each aligned block of 2048 tokens (one index of dp) holds either 2048 // 1024 sequences of 1024 tokens or 8 sequences of 256 tokens, numbered from 0 in order; exactly half of the blocks hold the long ones.
All inputs are finite; a program needn't handle non-finite values.
Results may differ from a plain program's by a relative error of at most 0.015.
The roundings to bfloat16 on the way count: a program that leaves them out, or rounds other values in their place, can miss the bound.
Values may be sent and summed in bfloat16 or wider, within the bound.
No kernel may reach another device: no remote copies, remote signals or barrier semaphores. Data moves between devices by JAX's collectives and lax.ppermute only.
A program may use at most 192 MiB of HBM per device.

v0:
```python
import math

import jax
import jax.numpy as jnp
from jax import lax
from jax.experimental import pallas as pl
from jax.experimental.pallas import tpu as pltpu
from jax.sharding import PartitionSpec as P


EPSILON = 1e-05
MASKED = -1e30
QUERY_ROWS = 256
SHORT_LEN = 256
BF16 = jnp.bfloat16
F32 = jnp.float32
VMEM_BYTES = 60 * 1024 * 1024


def dot_nn(left, right):
    return lax.dot_general(left, right, (((1,), (0,)), ((), ())), preferred_element_type=F32)


def dot_nt(left, right):
    return lax.dot_general(left, right, (((1,), (1,)), ((), ())), preferred_element_type=F32)


def normalize(values):
    row_mean = jnp.mean(values, axis=-1, keepdims=True)
    centered = values - row_mean
    inv_std = lax.rsqrt(jnp.mean(centered * centered, axis=-1, keepdims=True) + EPSILON)
    return (centered * inv_std, inv_std)


def norm_back(grad_normed, normed, inv_std, gain_vec):
    scaled = grad_normed * gain_vec
    return inv_std * (
        scaled
        - jnp.mean(scaled, axis=-1, keepdims=True)
        - normed * jnp.mean(scaled * normed, axis=-1, keepdims=True)
    )


def head_lanes(values, head, head_dim):
    per_group = 128 // head_dim
    first = (head // per_group) * 128
    group = values[:, first : min(first + 128, values.shape[1])]
    if group.shape[1] == head_dim:
        return group
    lane = lax.broadcasted_iota(jnp.int32, group.shape, 1)
    inside = (lane // head_dim) == (head % per_group)
    return jnp.where(inside, group, jnp.zeros_like(group))


def group_lanes(head, head_dim, width):
    per_group = 128 // head_dim
    first = (head // per_group) * 128
    return slice(first, min(first + 128, width))


def allowed_diagonal():
    key_pos = lax.broadcasted_iota(jnp.int32, (QUERY_ROWS, QUERY_ROWS), 0)
    row_pos = lax.broadcasted_iota(jnp.int32, (QUERY_ROWS, QUERY_ROWS), 1)
    return key_pos <= row_pos


def attend_block(queries, keys_ref, values_t_ref, start, old_blocks, heads, head_dim):
    width = heads * head_dim
    query_parts = [head_lanes(queries, head, head_dim) for head in range(heads)]

    def scores_of(head, rows):
        return dot_nt(keys_ref[rows, group_lanes(head, head_dim, width)], query_parts[head])

    def weighted(head, rows, weights):
        values_t = values_t_ref[head * head_dim : (head + 1) * head_dim, rows]
        return dot_nn(values_t, weights.astype(BF16))

    here = pl.ds(start, QUERY_ROWS)
    allowed = allowed_diagonal()
    state = []
    for head in range(heads):
        scores = jnp.where(allowed, scores_of(head, here), MASKED)
        row_max = jnp.max(scores, axis=0, keepdims=True)
        weights = jnp.exp(scores - row_max)
        state.append((row_max, jnp.sum(weights, axis=0, keepdims=True),
                      weighted(head, here, weights)))

    def old_block(index, state):
        rows = pl.ds(pl.multiple_of(index * QUERY_ROWS, QUERY_ROWS), QUERY_ROWS)
        result = []
        for head, (row_max, total, summed) in enumerate(state):
            scores = scores_of(head, rows)
            new_max = jnp.maximum(row_max, jnp.max(scores, axis=0, keepdims=True))
            weights = jnp.exp(scores - new_max)
            shrink = jnp.exp(row_max - new_max)
            result.append((new_max, total * shrink + jnp.sum(weights, axis=0, keepdims=True),
                           summed * shrink + weighted(head, rows, weights)))
        return tuple(result)

    state = lax.fori_loop(0, old_blocks, old_block, tuple(state))
    attended = jnp.concatenate([summed / total for _, total, summed in state], axis=0).T
    return attended, [row_max + jnp.log(total) for row_max, total, _ in state]


def attend_body(
    heads, head_dim, block, first_in, w_ref, bias_ref, mix_refs, att_ref, log_ref, keys_ref,
    values_t_ref, is_long,
):
    width = heads * head_dim
    projected = dot_nt(first_in, w_ref[...])
    queries = (projected[:, :width] + bias_ref[0:1, :]).astype(BF16)
    key_rows = projected[:, width : 2 * width].astype(BF16)
    value_rows = (projected[:, 2 * width :] + bias_ref[1:2, :]).astype(BF16)
    query_ref, key_ref, value_ref, keys_t_ref = mix_refs
    query_ref[...] = queries
    key_ref[...] = key_rows
    value_ref[...] = value_rows
    keys_t_ref[...] = key_rows.T
    start = pl.multiple_of(block * QUERY_ROWS, QUERY_ROWS)
    keys_ref[pl.ds(start, QUERY_ROWS), :] = key_rows
    values_t_ref[:, pl.ds(start, QUERY_ROWS)] = value_rows.T
    scaled = queries * jnp.asarray(1.0 / math.sqrt(head_dim), BF16)

    attended, logs = attend_block(
        scaled, keys_ref, values_t_ref, start, block * is_long, heads, head_dim
    )
    att_ref[...] = attended.astype(BF16)
    log_ref[...] = jnp.concatenate(logs + [jnp.zeros((8 - heads, QUERY_ROWS), F32)], axis=0)


def forward_own_kernel(heads, head_dim, info_ref, x_ref, gain_ref, shift_ref, w_ref, bias_ref,
                       first_ref, first_t_ref, query_ref, key_ref, value_ref, keys_t_ref, att_ref,
                       log_ref, keys_ref, values_t_ref):
    normed, _ = normalize(x_ref[...].astype(F32))
    first_in = (normed * gain_ref[...] + shift_ref[...]).astype(BF16)
    first_ref[...] = first_in
    first_t_ref[...] = first_in.T
    attend_body(heads, head_dim, pl.program_id(0), first_in, w_ref, bias_ref,
                (query_ref, key_ref, value_ref, keys_t_ref), att_ref, log_ref, keys_ref,
                values_t_ref, info_ref[1])


def forward_other_kernel(heads, head_dim, info_ref, first_ref, w_ref, bias_ref, att_own_ref,
                         w_out_own_ref, w_out_ref, query_ref, key_ref, value_ref, keys_t_ref,
                         att_ref, log_ref, branch_ref, keys_ref, values_t_ref):
    attend_body(heads, head_dim, pl.program_id(0), first_ref[...], w_ref, bias_ref,
                (query_ref, key_ref, value_ref, keys_t_ref), att_ref, log_ref, keys_ref,
                values_t_ref, info_ref[1])
    branch = dot_nn(att_own_ref[...], w_out_own_ref[...]) + dot_nn(att_ref[...], w_out_ref[...])
    branch_ref[...] = branch.astype(BF16)


def write_split(source_ref, kept_ref, sent_ref, mine, part=None):
    run = kept_ref.shape[-2]
    count = kept_ref.shape[-3]
    for value in range(2):

        @pl.when(mine == value)
        def _(value=value):
            for index in range(2 * count):
                target = kept_ref if index % 2 == value else sent_ref
                piece = source_ref[index * run : (index + 1) * run, :].astype(BF16)
                if part is None:
                    target[index // 2] = piece
                else:
                    target[part, index // 2] = piece


def mlp_kernel(info_ref, x_ref, branch_a_ref, branch_b_ref, b_out_ref, gain_ref, shift_ref, go_ref,
               fc_own_ref, fc_top_ref, fc_low_ref, proj_own_ref, proj_other_ref, b_fc_ref,
               residual_ref, mlp_ref, grad_ref, fc_kept_ref, fc_sent_ref, proj_kept_ref,
               proj_sent_ref, d_b_fc_ref, d_b_proj_ref,
               in_t_ref, go_t_ref, pre_own_ref, pre_other_ref, act_own_ref, act_other_ref):
    step = pl.program_id(0)
    rows = x_ref.shape[0]

    @pl.when(step == 0)
    def _():
        d_b_fc_ref[...] = jnp.zeros_like(d_b_fc_ref)
        d_b_proj_ref[...] = jnp.zeros_like(d_b_proj_ref)

    residual = x_ref[...].astype(F32) + (
        branch_a_ref[...].astype(F32) + branch_b_ref[...].astype(F32) + b_out_ref[...]
    )
    residual_ref[...] = residual
    normed, _ = normalize(residual)
    second_in = (normed * gain_ref[...] + shift_ref[...]).astype(BF16)
    grad_out = go_ref[...]
    here = pl.ds(pl.multiple_of(step * rows, rows), rows)
    in_t_ref[:, here] = second_in.T
    go_t_ref[:, here] = grad_out.T

    d_b_proj_ref[...] += jnp.sum(grad_out.astype(F32), axis=0, keepdims=True)
    mlp = None
    grad_second = None
    grad_acts = [dot_nt(grad_out, ref[...]) for ref in (proj_own_ref, proj_other_ref)]
    parts = (
        ((fc_own_ref,), proj_own_ref, pre_own_ref, act_own_ref),
        ((fc_top_ref, fc_low_ref), proj_other_ref, pre_other_ref, act_other_ref),
    )
    slope = math.sqrt(2.0 / math.pi)
    for part, (fc_refs, proj_ref, pre_ref, act_ref) in enumerate(parts):
        pre_act = b_fc_ref[part : part + 1, :]
        first = 0
        for fc_ref in fc_refs:
            last = first + fc_ref.shape[0]
            pre_act = pre_act + dot_nn(second_in[:, first:last], fc_ref[...])
            first = last
        square = pre_act * pre_act
        bent = jnp.tanh(pre_act * (slope + (0.044715 * slope) * square))
        half = 0.5 + 0.5 * bent
        act_low = (pre_act * half).astype(BF16)
        act_ref[here, :] = act_low
        part_out = dot_nn(act_low, proj_ref[...])
        grad_act = grad_acts[part]
        rise = pre_act * (2.0 * slope + (6.0 * 0.044715 * slope) * square)
        derivative = half + half * ((1.0 - half) * rise)
        grad_pre = (grad_act * derivative).astype(BF16)
        pre_ref[here, :] = grad_pre
        d_b_fc_ref[part : part + 1, :] += jnp.sum(grad_pre.astype(F32), axis=0, keepdims=True)
        part_grad = jnp.concatenate([dot_nt(grad_pre, fc_ref[...]) for fc_ref in fc_refs], axis=1)
        mlp = part_out if mlp is None else mlp + part_out
        grad_second = part_grad if grad_second is None else grad_second + part_grad
    mlp_ref[...] = mlp.astype(BF16)
    grad_ref[...] = grad_second.astype(BF16)

    @pl.when(step == pl.num_programs(0) - 1)
    def _():
        for part, (act_ref, pre_ref) in enumerate(
            ((act_own_ref, pre_own_ref), (act_other_ref, pre_other_ref))
        ):
            write_split(dot_nn(in_t_ref[...], pre_ref[...]).astype(BF16), fc_kept_ref,
                        fc_sent_ref, info_ref[5], part)
            write_split(dot_nn(go_t_ref[...], act_ref[...]).astype(BF16), proj_kept_ref,
                        proj_sent_ref, info_ref[6], part)


def attend_back_block(queries, grads, attended, logs, keys_ref, keys_t_ref, values_ref,
                      grad_keys_ref, grad_values_ref, start, old_blocks, heads, head_dim, scale):
    width = heads * head_dim
    query_parts = [head_lanes(queries, head, head_dim) for head in range(heads)]
    scaled_parts = [query * jnp.asarray(scale, BF16) for query in query_parts]
    grad_parts = [head_lanes(grads, head, head_dim) for head in range(heads)]
    product = grads.astype(F32) * attended.astype(F32)
    high = product.astype(BF16)
    low = (product - high.astype(F32)).astype(BF16)
    member = (
        lax.broadcasted_iota(jnp.int32, (8, width), 1) // head_dim
        == lax.broadcasted_iota(jnp.int32, (8, width), 0)
    )
    member = jnp.where(member, 1.0, 0.0).astype(BF16)
    deltas = dot_nt(member, high) + dot_nt(member, low)

    def through(rows, allowed):
        results = []
        for head in range(heads):
            lanes = group_lanes(head, head_dim, width)
            scores = dot_nt(keys_ref[rows, lanes], scaled_parts[head])
            weights = jnp.exp(scores - logs[head : head + 1, :])
            if allowed is not None:
                weights = jnp.where(allowed, weights, 0.0)
            grad_weights = dot_nt(values_ref[rows, lanes], grad_parts[head])
            grad_scores = (weights * (grad_weights - deltas[head : head + 1, :])).astype(BF16)
            grad_keys_ref[rows, lanes] += dot_nn(grad_scores, query_parts[head])
            grad_values_ref[rows, lanes] += dot_nn(weights.astype(BF16), grad_parts[head])
            keys_t = keys_t_ref[head * head_dim : (head + 1) * head_dim, rows]
            results.append(dot_nn(keys_t, grad_scores))
        return tuple(results)

    def old_block(index, sums):
        rows = pl.ds(pl.multiple_of(index * QUERY_ROWS, QUERY_ROWS), QUERY_ROWS)
        return tuple(old + new for old, new in zip(sums, through(rows, None)))

    sums = through(pl.ds(start, QUERY_ROWS), allowed_diagonal())
    sums = lax.fori_loop(0, old_blocks, old_block, sums)
    return jnp.concatenate(sums, axis=0).T * scale


def backward_other_kernel(heads, head_dim, info_ref, grad_a_ref, grad_b_ref, residual_ref, go_ref,
                          gain_ref, mlp_a_ref, mlp_b_ref, b_proj_ref, query_ref, key_ref, value_ref,
                          keys_t_ref, att_ref, log_ref, w_ref, w_out_ref, first_t_hbm,
                          grad_residual_ref, grad_branch_ref, grad_branch_t_ref, grad_first_ref,
                          kept_ref, sent_ref, d_bias_ref, d_norm_ref, block_ref,
                          first_t_ref, mixed_ref, grad_keys_ref, grad_values_ref, copy_sem):
    step = pl.program_id(0)
    copies = (pltpu.make_async_copy(first_t_hbm, first_t_ref, copy_sem.at[0]),)

    @pl.when(step == 0)
    def _():
        copies[0].start()
        d_norm_ref[...] = jnp.zeros_like(d_norm_ref)
        grad_keys_ref[...] = jnp.zeros_like(grad_keys_ref)
        grad_values_ref[...] = jnp.zeros_like(grad_values_ref)
        d_bias_ref[...] = jnp.zeros_like(d_bias_ref)

    rows = grad_a_ref.shape[0]
    block = pl.num_programs(0) - 1 - step
    here = pl.ds(pl.multiple_of(block * rows, rows), rows)
    grad_second = grad_a_ref[...].astype(F32) + grad_b_ref[...].astype(F32)
    normed, inv_std = normalize(residual_ref[...])
    grad_residual = go_ref[...].astype(F32) + norm_back(grad_second, normed, inv_std, gain_ref[...])
    grad_residual_ref[...] = grad_residual
    block_ref[...] = block_value(residual_ref, mlp_a_ref, mlp_b_ref, b_proj_ref)
    grad_branch = grad_residual.astype(BF16)
    grad_branch_ref[...] = grad_branch
    grad_branch_t_ref[:, here] = grad_branch.T
    d_norm_ref[0:1, :] += jnp.sum(grad_second * normed, axis=0, keepdims=True)
    d_norm_ref[1:2, :] += jnp.sum(grad_second, axis=0, keepdims=True)
    d_norm_ref[2:3, :] += jnp.sum(grad_branch.astype(F32), axis=0, keepdims=True)
    grad_first_ref[...] = attend_back(
        heads, head_dim, grad_branch, query_ref, key_ref, value_ref, keys_t_ref, att_ref, log_ref,
        w_ref, w_out_ref, d_bias_ref, mixed_ref, grad_keys_ref, grad_values_ref, info_ref[1])
    weight_grads(copies, first_t_ref, grad_branch_t_ref, mixed_ref, att_ref,
                 kept_ref, sent_ref, info_ref[5])


def backward_own_kernel(heads, head_dim, info_ref, grad_branch_ref, grad_first_in_ref, query_ref,
                        key_ref, value_ref, keys_t_ref, att_ref, log_ref, w_ref, w_out_ref,
                        first_t_hbm, grad_branch_t_hbm, grad_first_ref, kept_ref, sent_ref,
                        d_bias_ref, first_t_ref, grad_branch_t_ref, mixed_ref, grad_keys_ref,
                        grad_values_ref, copy_sem):
    copies = (
        pltpu.make_async_copy(first_t_hbm, first_t_ref, copy_sem.at[0]),
        pltpu.make_async_copy(grad_branch_t_hbm, grad_branch_t_ref, copy_sem.at[1]),
    )

    @pl.when(pl.program_id(0) == 0)
    def _():
        for copy in copies:
            copy.start()
        grad_keys_ref[...] = jnp.zeros_like(grad_keys_ref)
        grad_values_ref[...] = jnp.zeros_like(grad_values_ref)
        d_bias_ref[...] = jnp.zeros_like(d_bias_ref)

    grad_first = attend_back(
        heads, head_dim, grad_branch_ref[...], query_ref, key_ref, value_ref, keys_t_ref, att_ref,
        log_ref, w_ref, w_out_ref, d_bias_ref, mixed_ref, grad_keys_ref, grad_values_ref,
        info_ref[1])
    grad_first_ref[...] = (grad_first + grad_first_in_ref[...]).astype(BF16)
    weight_grads(copies, first_t_ref, grad_branch_t_ref, mixed_ref, att_ref,
                 kept_ref, sent_ref, info_ref[5])


def attend_back(heads, head_dim, grad_branch, query_ref, key_ref, value_ref, keys_t_ref, att_ref,
                log_ref, w_ref, w_out_ref, d_bias_ref, mixed_ref, grad_keys_ref, grad_values_ref,
                is_long):
    blocks = key_ref.shape[0] // QUERY_ROWS
    block = blocks - 1 - pl.program_id(0)
    scale = 1.0 / math.sqrt(head_dim)
    start = pl.multiple_of(block * QUERY_ROWS, QUERY_ROWS)
    here = pl.ds(start, QUERY_ROWS)
    grads = dot_nt(grad_branch, w_out_ref[...]).astype(BF16)
    grad_queries = attend_back_block(
        query_ref[...], grads, att_ref[here, :], log_ref[...], key_ref, keys_t_ref, value_ref,
        grad_keys_ref, grad_values_ref, start, block * is_long, heads, head_dim, scale)
    mixed = jnp.concatenate(
        [grad_queries.astype(BF16), (grad_keys_ref[here, :] * scale).astype(BF16),
         grad_values_ref[here, :].astype(BF16)], axis=1
    )
    mixed_ref[here, :] = mixed
    d_bias_ref[...] += jnp.sum(mixed.astype(F32), axis=0, keepdims=True)
    return dot_nn(mixed, w_ref[...])


def weight_grads(copies, first_t_ref, grad_branch_t_ref, mixed_ref, att_ref, kept_ref,
                 sent_ref, mine):
    @pl.when(pl.program_id(0) == pl.num_programs(0) - 1)
    def _():
        for copy in copies:
            copy.wait()
        total = jnp.concatenate(
            [dot_nn(first_t_ref[...], mixed_ref[...]).astype(BF16),
             dot_nn(grad_branch_t_ref[...], att_ref[...]).astype(BF16)], axis=1
        )
        write_split(total, kept_ref, sent_ref, mine)


def last_norm_kernel(info_ref, x_ref, grad_a_ref, grad_b_ref, grad_residual_ref, gain_ref,
                     d_b_proj_ref, d_norm_two_ref, d_b_fc_ref, bias_own_ref, bias_other_ref,
                     grad_in_ref, near_ref, small_ref, sent_ref):
    step = pl.program_id(0)
    local = bias_own_ref.shape[1] // 3

    @pl.when(step == 0)
    def _():
        for target, row, bias_ref in ((small_ref, 0, bias_own_ref), (sent_ref, 1, bias_other_ref)):
            target[...] = jnp.zeros_like(target)
            target[0:1, :] = d_b_proj_ref[...]
            target[1:4, :] = d_norm_two_ref[0:3, :]
            target[6:7, :] = d_b_fc_ref[row : row + 1, :]
            target[7:8, 0 : 2 * local] = jnp.concatenate(
                [bias_ref[:, 0:local], bias_ref[:, 2 * local :]], axis=1
            )

    grad_first = grad_a_ref[...].astype(F32) + grad_b_ref[...].astype(F32)
    normed, inv_std = normalize(x_ref[...].astype(F32))
    grad_in = grad_residual_ref[...] + norm_back(grad_first, normed, inv_std, gain_ref[...])
    grad_low = grad_in.astype(BF16)
    grad_in_ref[...] = grad_low.astype(F32)

    @pl.when((step * x_ref.shape[0]) // info_ref[4] == info_ref[2])
    def _():
        near_ref[...] = grad_low

    gain_sum = jnp.sum(grad_first * normed, axis=0, keepdims=True)
    shift_sum = jnp.sum(grad_first, axis=0, keepdims=True)
    for target in (small_ref, sent_ref):
        target[4:5, :] += gain_sum
        target[5:6, :] += shift_sum


def block_value(residual_ref, mlp_a_ref, mlp_b_ref, bias_ref):
    total = residual_ref[...] + (mlp_a_ref[...].astype(F32) + mlp_b_ref[...].astype(F32))
    return (total + bias_ref[...]).astype(BF16)


def block_half_kernel(info_ref, residual_ref, mlp_a_ref, mlp_b_ref, bias_ref, out_ref):
    out_ref[...] = block_value(residual_ref, mlp_a_ref, mlp_b_ref, bias_ref)


def fill_both_kernel(info_ref, near_ref, far_ref, whole_ref, out_ref):
    from_near = (pl.program_id(0) * near_ref.shape[0]) // info_ref[4] == info_ref[2]
    out_ref[...] = jnp.where(from_near, near_ref[...], far_ref[...]).astype(out_ref.dtype)


def row_spec(rows, width, shift=False):
    if shift:
        return pl.BlockSpec((rows, width), lambda step, info: (info[0] + step, 0))
    return pl.BlockSpec((rows, width), lambda step, info: (step, 0))


def back_spec(rows, width, blocks, shift=False):
    if shift:
        return pl.BlockSpec((rows, width), lambda step, info: (info[0] + blocks - 1 - step, 0))
    return pl.BlockSpec((rows, width), lambda step, info: (blocks - 1 - step, 0))


def whole(shape):
    return pl.BlockSpec(shape, lambda step, info: (0,) * len(shape))


def call(kernel, steps, in_specs, out_specs, out_shape, scratch, cost_us, aliases=None):
    return pl.pallas_call(
        kernel,
        grid_spec=pltpu.PrefetchScalarGridSpec(
            num_scalar_prefetch=1,
            grid=(steps,),
            in_specs=in_specs,
            out_specs=out_specs,
            scratch_shapes=scratch,
        ),
        out_shape=out_shape,
        input_output_aliases=aliases or {},
        compiler_params=pltpu.CompilerParams(
            dimension_semantics=("arbitrary",), vmem_limit_bytes=VMEM_BYTES
        ),
        cost_estimate=pl.CostEstimate(
            flops=int(cost_us * 1e9), transcendentals=0, bytes_accessed=int(cost_us * 3e6)
        ),
    )


def struct(shape, dtype):
    return jax.ShapeDtypeStruct(shape, dtype)


def exchange(value, axis_name, size, bit):
    return lax.ppermute(value, axis_name, [(i, i ^ bit) for i in range(size)])


def after(value, earlier):
    return lax.optimization_barrier((value, earlier))[0]


def make_body(dp_size, tensor_size):
    def body(hidden_in, doc_ids, ln1_gain, ln1_bias, w_qkv, b_qv, w_out, b_out, ln2_gain, ln2_bias,
             w_fc, b_fc, w_proj, b_proj, grad_out):
        row_count, width = hidden_in.shape
        heads, head_dim = w_qkv.shape[2:]
        local = heads * head_dim
        hidden = w_fc.shape[1]
        rows = row_count // 2
        blocks = rows // QUERY_ROWS
        half = rows // 2
        place = lax.axis_index("tensor")
        bits = dp_size.bit_length() - 1
        position = lax.axis_index("dp")
        share = width // dp_size
        first_bit = next(bit for bit in range(bits) if (share << bit) % 16 == 0)
        second_bit = min(first_bit + 1, bits - 1)
        upper = place // 2
        core = place % 2
        is_long = (doc_ids[SHORT_LEN] == doc_ids[0]).astype(jnp.int32)
        info = jnp.stack(
            [upper * blocks, is_long, core, (1 - upper) * blocks, half,
             (position >> first_bit) & 1, (position >> second_bit) & 1]
        ).astype(jnp.int32)

        def core_swap(value):
            return exchange(value, "tensor", tensor_size, 1)

        def pair_swap(value):
            return exchange(value, "tensor", tensor_size, 2)

        qkv_own = w_qkv.transpose(1, 2, 3, 0).reshape(3 * local, width)
        out_own = w_out.reshape(local, width)
        bias_own = b_qv.reshape(2, local)
        small_other = pair_swap(
            jnp.concatenate([b_qv.reshape(1, 2 * local), b_fc.reshape(1, hidden)], axis=1)
        )

        def my_piece(matrix):
            rows_each = matrix.shape[0] // dp_size
            return lax.dynamic_slice_in_dim(matrix, position * rows_each, rows_each, axis=0)[None]

        def widen(kept, come, bit):
            mine = (position >> bit) & 1
            return tuple(
                jnp.where(mine == 0, jnp.stack([a, b], 1), jnp.stack([b, a], 1)).reshape(
                    (2 * a.shape[0],) + a.shape[1:]
                )
                for a, b in zip(kept, come)
            )

        def dp_swap(values, bit):
            return tuple(exchange(value, "dp", dp_size, 1 << bit) for value in values)

        parts = tuple(
            pair_swap(my_piece(matrix)) for matrix in (w_proj, w_fc[width // 2 :])
        )
        out_other = pair_swap(out_own)
        qkv_other = pair_swap(qkv_own)
        fc_top = pair_swap(w_fc[: width // 2])
        come = dp_swap(parts, bits - 1)
        come, hidden_in = lax.optimization_barrier((come, hidden_in))
        parts = widen(parts, come, bits - 1)
        come = dp_swap(parts, bits - 2)

        first_spec = row_spec(QUERY_ROWS, width)
        turned_spec = pl.BlockSpec((local, QUERY_ROWS), lambda step, info: (0, step))
        att_spec = row_spec(QUERY_ROWS, local)
        log_spec = pl.BlockSpec((8, QUERY_ROWS), lambda step, info: (0, step))
        mix_specs = [att_spec] * 3 + [turned_spec]
        mix_structs = [struct((rows, local), BF16)] * 3 + [struct((local, rows), BF16)]
        attend_scratch = [pltpu.VMEM((rows, local), BF16), pltpu.VMEM((local, rows), BF16)]

        def forward_own(*refs):
            forward_own_kernel(heads, head_dim, *refs)

        def forward_other(*refs):
            forward_other_kernel(heads, head_dim, *refs)

        first_in, first_t, *mix_own, att_own, log_own = call(
            forward_own,
            blocks,
            [row_spec(QUERY_ROWS, width, True), whole((width,)), whole((width,)),
             whole((3 * local, width)), whole((2, local))],
            [first_spec, pl.BlockSpec((width, QUERY_ROWS), lambda step, info: (0, step))]
            + mix_specs + [att_spec, log_spec],
            [struct((rows, width), BF16), struct((width, rows), BF16)] + mix_structs
            + [struct((rows, local), BF16), struct((8, rows), F32)],
            attend_scratch,
            11,
        )(info, hidden_in, ln1_gain, ln1_bias, qkv_own, bias_own)
        come, small_other = after((come, small_other), first_in)
        parts = widen(parts, come, bits - 2)
        for bit in reversed(range(bits - 2)):
            come = dp_swap(parts, bit)
            if bit:
                first_in = after(first_in, come)
            parts = widen(parts, come, bit)
        proj_other = parts[0].reshape(hidden, width)
        fc_low = parts[1].reshape(width // 2, hidden)
        bias_other = small_other[:, : 2 * local].reshape(2, local)
        b_fc_both = jnp.concatenate([b_fc.reshape(1, hidden), small_other[:, 2 * local :]], axis=0)
        *mix_other, att_other, log_other, branch = call(
            forward_other,
            blocks,
            [first_spec, whole((3 * local, width)), whole((2, local)), att_spec,
             whole((local, width)), whole((local, width))],
            mix_specs + [att_spec, log_spec, first_spec],
            mix_structs + [struct((rows, local), BF16), struct((8, rows), F32),
                           struct((rows, width), BF16)],
            attend_scratch,
            12,
        )(info, first_in, qkv_other, bias_other, att_own, out_own, out_other)
        branch_swapped = core_swap(branch)

        def split_shape(bit, lead=()):
            runs = dp_size >> bit
            return lead + (runs // 2, share << bit, width)

        fc_shape = split_shape(first_bit, (2,))
        proj_shape = split_shape(second_bit, (2,))
        att_shape = split_shape(first_bit)
        (residual, mlp, grad_second, fc_kept, fc_sent, proj_kept, proj_sent, d_b_fc,
         d_b_proj) = call(
            mlp_kernel,
            blocks,
            [row_spec(QUERY_ROWS, width, True), first_spec, first_spec, whole((width,)),
             whole((width,)), whole((width,)), row_spec(QUERY_ROWS, width, True),
             whole((width, hidden)), whole((width // 2, hidden)), whole((width // 2, hidden)),
             whole((hidden, width)), whole((hidden, width)), whole((2, hidden))],
            [first_spec, first_spec, first_spec] + [whole(fc_shape)] * 2 + [whole(proj_shape)] * 2
            + [whole((2, hidden)), whole((1, width))],
            [struct((rows, width), F32), struct((rows, width), BF16), struct((rows, width), BF16),
             struct(fc_shape, BF16), struct(fc_shape, BF16), struct(proj_shape, BF16),
             struct(proj_shape, BF16),
             struct((2, hidden), F32), struct((1, width), F32)],
            [pltpu.VMEM((width, rows), BF16)] * 2 + [pltpu.VMEM((rows, hidden), BF16)] * 4,
            28,
        )(info, hidden_in, branch, branch_swapped, b_out, ln2_gain,
          ln2_bias, grad_out, w_fc, fc_top, fc_low, w_proj, proj_other, b_fc_both)
        grad_swapped = core_swap(grad_second)
        mlp_swapped = core_swap(mlp)

        half_spec = pl.BlockSpec(
            (QUERY_ROWS, width), lambda step, info: (info[2] * (half // QUERY_ROWS) + step, 0)
        )
        block_half = call(
            block_half_kernel,
            half // QUERY_ROWS,
            [half_spec, half_spec, half_spec, whole((width,))],
            first_spec,
            struct((half, width), BF16),
            [],
            3,
        )(info, residual, mlp, mlp_swapped, b_proj)
        block_near = pair_swap(block_half)

        back_rows = back_spec(QUERY_ROWS, width, blocks)
        back_att = back_spec(QUERY_ROWS, local, blocks)
        back_log = pl.BlockSpec((8, QUERY_ROWS), lambda step, info: (0, blocks - 1 - step))
        back_scratch = [
            pltpu.VMEM((rows, 3 * local), BF16),
            pltpu.VMEM((rows, local), F32),
            pltpu.VMEM((rows, local), F32),
            pltpu.SemaphoreType.DMA((2,)),
        ]
        turned_scratch = pltpu.VMEM((width, rows), BF16)
        back_mix = [back_att, whole((rows, local)), whole((rows, local)), whole((local, rows)),
                    whole((rows, local)), back_log, whole((3 * local, width)),
                    whole((local, width))]
        in_place = pl.BlockSpec(memory_space=pl.ANY)

        def backward_other(*refs):
            backward_other_kernel(heads, head_dim, *refs)

        def backward_own(*refs):
            backward_own_kernel(heads, head_dim, *refs)

        (grad_residual, grad_branch, grad_branch_t, grad_first_other, far_kept, far_sent, d_bias_other,
         d_norm_two, block_out) = call(
            backward_other,
            blocks,
            [back_rows, back_rows, back_rows, back_spec(QUERY_ROWS, width, blocks, True),
             whole((width,)), back_rows, back_rows, whole((width,))] + back_mix + [in_place],
            [back_rows, back_rows, whole((width, rows)), back_rows, whole(att_shape), whole(att_shape),
             whole((1, 3 * local)), whole((8, width)),
             back_spec(QUERY_ROWS, width, blocks, True)],
            [struct((rows, width), F32), struct((rows, width), BF16),
             struct((width, rows), BF16), struct((rows, width), F32),
             struct(att_shape, BF16), struct(att_shape, BF16), struct((1, 3 * local), F32),
             struct((8, width), F32), struct((row_count, width), BF16)],
            [turned_scratch] + back_scratch,
            21,
        )(info, grad_second, grad_swapped, residual, grad_out, ln2_gain, mlp, mlp_swapped, b_proj,
          *mix_other, att_other, log_other, qkv_other, out_other, first_t)
        grad_first, near_kept, near_sent, d_bias_own = call(
            backward_own,
            blocks,
            [back_rows, back_rows] + back_mix + [in_place, in_place],
            [back_rows, whole(att_shape), whole(att_shape), whole((1, 3 * local))],
            [struct((rows, width), BF16), struct(att_shape, BF16), struct(att_shape, BF16),
             struct((1, 3 * local), F32)],
            [turned_scratch, turned_scratch] + back_scratch,
            17,
        )(info, grad_branch, grad_first_other, *mix_own, att_own, log_own, qkv_own, out_own,
          first_t, grad_branch_t)
        first_swapped = core_swap(grad_first)
        quarter = half // QUERY_ROWS
        small_spec = whole((8, width))
        grad_in, grad_half, small, small_sent = call(
            last_norm_kernel,
            blocks,
            [row_spec(QUERY_ROWS, width, True), first_spec, first_spec, first_spec,
             whole((width,)), whole((1, width)), small_spec, whole((2, hidden)),
             whole((1, 3 * local)), whole((1, 3 * local))],
            [row_spec(QUERY_ROWS, width, True),
             pl.BlockSpec((QUERY_ROWS, width), lambda step, info: (
                jnp.clip(step - quarter * info[2], 0, quarter - 1), 0)),
             small_spec, small_spec],
            [struct((row_count, width), F32), struct((half, width), BF16),
             struct((8, width), F32), struct((8, width), F32)],
            [],
            7,
        )(info, hidden_in, grad_first, first_swapped, grad_residual, ln1_gain, d_b_proj,
          d_norm_two, d_b_fc, d_bias_own, d_bias_other)
        small_come = pair_swap(small_sent)
        grad_near = pair_swap(grad_half)

        def quarter_spec(part):
            def index(step, info):
                first = jnp.where(part == 0, info[2], 1 - info[2]) * quarter
                return jnp.clip(step - first, 0, quarter - 1), 0

            return pl.BlockSpec((QUERY_ROWS, width), index)

        def fill_both(target, near, far):
            return call(
                fill_both_kernel,
                blocks,
                [quarter_spec(0), quarter_spec(1), pl.BlockSpec(memory_space=pl.ANY)],
                pl.BlockSpec((QUERY_ROWS, width), lambda step, info: (info[3] + step, 0)),
                struct(target.shape, target.dtype),
                [],
                3,
                {3: 0},
            )(info, near, far, target)

        block_far = core_swap(block_near)
        block_near, block_far = after((block_near, block_far), grad_half)
        block_out = fill_both(block_out, block_near, block_far)
        grad_far = core_swap(grad_near)
        grad_in = fill_both(grad_in, grad_near, grad_far)

        def pick(value, axis, which):
            return lax.dynamic_index_in_dim(value, which, axis, keepdims=False)

        def parted(value, lead=()):
            return value.reshape(lead + (2,) * (bits - 1) + (share, width))

        def add(kept, received):
            return kept.astype(F32) + received.astype(F32)

        def others(bit):
            return [b for b in range(bits) if b != bit]

        def stages(value, left):
            for number, bit in enumerate(left):
                above = len([b for b in left[number:] if b > bit])
                mine = (position >> bit) & 1
                received = exchange(
                    pick(value, above, 1 - mine).astype(BF16), "dp", dp_size, 1 << bit
                )
                if number == 0:
                    received = after(received, grad_half)
                value = add(pick(value, above, mine), received)
            return value

        got_fc = exchange(fc_sent, "dp", dp_size, 1 << first_bit)
        got_proj = exchange(proj_sent, "dp", dp_size, 1 << second_bit)
        got_far = exchange(far_sent, "dp", dp_size, 1 << first_bit)
        got_fc, got_proj = after((got_fc, got_proj), grad_branch)
        half_fc = add(fc_kept, got_fc)
        half_proj = add(proj_kept, got_proj)
        come_fc = pair_swap(half_fc[1].astype(BF16))
        come_proj = pair_swap(half_proj[1].astype(BF16))
        got_near = exchange(near_sent, "dp", dp_size, 1 << first_bit)
        got_far = after(got_far, grad_first)
        come_far = pair_swap(add(far_kept, got_far).astype(BF16))
        come_fc = after(come_fc, grad_first)
        come_proj, come_far, got_near = after((come_proj, come_far, got_near), grad_half)
        fc_share = stages(parted(add(half_fc[0], come_fc)), others(first_bit))
        proj_share = stages(parted(add(half_proj[0], come_proj)), others(second_bit))
        att_half = parted(add(add(near_kept, got_near), come_far))
        att_share = stages(att_half, others(first_bit))
        small = small + small_come
        for bit in range(bits):
            small_come = exchange(small, "dp", dp_size, 1 << bit)
            small = small + small_come
        shares = lax.dynamic_index_in_dim(
            small[0:6].reshape(6, dp_size, share), position, 1, keepdims=False
        )
        d_b_proj_share, d_gain_two, d_shift_two, d_b_out, d_gain_one, d_shift_one = (
            shares[i] for i in range(6)
        )
        fc_rows, fc_columns = b_fc.shape
        d_b_fc_share = lax.dynamic_slice_in_dim(
            small[6].reshape(fc_rows, fc_columns), position * (fc_columns // dp_size),
            fc_columns // dp_size, axis=1,
        )
        d_b_qv_share = lax.dynamic_slice_in_dim(
            small[7, : 2 * local].reshape(2, heads, head_dim), position * (head_dim // dp_size),
            head_dim // dp_size, axis=2,
        )
        att_turned = att_share.T
        d_w_qkv = att_turned[: 3 * local].reshape(3, heads, head_dim, share).transpose(3, 0, 1, 2)
        d_w_out = att_turned[3 * local :].reshape(heads, head_dim, share)
        return (block_out, grad_in, d_gain_one, d_shift_one, d_w_qkv, d_b_qv_share, d_w_out,
                d_b_out, d_gain_two, d_shift_two, fc_share, d_b_fc_share, proj_share.T,
                d_b_proj_share)

    return body


def solution(mesh):
    in_specs = (
        P("dp", None),
        P("dp"),
        P(),
        P(),
        P(None, None, "tensor", None),
        P(None, "tensor", None),
        P("tensor", None, None),
        P(),
        P(),
        P(),
        P(None, "tensor"),
        P("tensor", None),
        P("tensor", None),
        P(),
        P("dp", None),
    )
    out_specs = (
        P("dp", None),
        P("dp", None),
        P("dp"),
        P("dp"),
        P("dp", None, "tensor", None),
        P(None, "tensor", "dp"),
        P("tensor", None, "dp"),
        P("dp"),
        P("dp"),
        P("dp"),
        P("dp", "tensor"),
        P("tensor", "dp"),
        P("tensor", "dp"),
        P("dp"),
    )
    inner = make_body(mesh.shape["dp"], mesh.shape["tensor"])

    return jax.shard_map(inner, mesh=mesh, in_specs=in_specs, out_specs=out_specs, check_vma=False)
```

profile of v0, /device:TPU:0, one launch (start us, length us, event | category | flops | bytes accessed | tf_op | source)
XLA Modules:
  0.0 281.5 jit_solution(6557219939638060522)
XLA Ops:
  0.6 0.9 dynamic-slice_bitcast_fusion
  1.6 3.1 %collective-permute-start = (bf16[1,96,768]{2,1,0:T(8,128)(2,1)S(1)}, bf16[1,96,768]{2,1,0:T(8,128)(2,1)S(1)}, u32[]{:S(2)}, u32[]{:S(2)}) collective-permute-start(bf16[1,96,768]{2,1,0:T(8,128)(2,1)S(1)} %dynamic-slice_bitcast_fusion), channel_id=1, source_target_pairs={{0,2},{1,3},{2,0},{3,1},{4,6},{5,7},{6,4},{7,5},{8,10},{9,11},{10,... | collective-permute-start | bytes 442376 | tf_op jit(solution)/shard_map/ppermute | solution.py:468
  4.7 1.3 fusion.18
  6.3 2.5 collective-permute-done
  8.8 3.0 %collective-permute-start.1 = (bf16[1,96,768]{2,1,0:T(8,128)(2,1)S(1)}, bf16[1,96,768]{2,1,0:T(8,128)(2,1)S(1)}, u32[]{:S(2)}, u32[]{:S(2)}) collective-permute-start(bf16[1,96,768]{2,1,0:T(8,128)(2,1)S(1)} %collective-permute-done), channel_id=1, source_target_pairs={{0,16},{4,20},{8,24},{12,28},{16,0},{20,4},{24,8},{28,12},{1,17},{... | collective-permute-start | bytes 442376 | tf_op jit(solution)/shard_map/ppermute | solution.py:468
  11.8 1.8 collective-permute-start.7
  13.9 1.8 collective-permute-start.8
  16.7 1.3 fusion.19
  19.8 1.7 collective-permute-done.3
  21.6 1.6 collective-permute-start.6
  23.8 15.0 %shard_map.254 = (bf16[1024,768]{1,0:T(8,128)(2,1)}, bf16[768,1024]{1,0:T(8,128)(2,1)}, bf16[1024,192]{1,0:T(8,128)(2,1)}, bf16[1024,192]{1,0:T(8,128)(2,1)}, bf...) custom-call(s32[7]{0:T(128)} %stack.100.refs_0_.info_ref, ...), custom_call_target="tpu_custom_call" | custom-call | flops 11000000512 | bytes 33000000 | tf_op jit(solution)/shard_map/pallas_call | solution.py:553
  39.6 0.9 copy-done.16
  40.5 15.4 %shard_map.255 = (bf16[1024,192]{1,0:T(8,128)(2,1)}, bf16[1024,192]{1,0:T(8,128)(2,1)}, bf16[1024,192]{1,0:T(8,128)(2,1)}, bf16[192,1024]{1,0:T(8,128)(2,1)}, bf...) custom-call(s32[7]{0:T(128)} %stack.100.refs_0_.info_ref, ...), custom_call_target="tpu_custom_call" | custom-call | flops 12000000000 | bytes 36000000 | tf_op jit(solution)/shard_map/pallas_call | solution.py:576
  56.4 1.6 collective-permute-start.12
  59.2 19.0 %collective-permute-done.11 = bf16[4,48,768]{2,1,0:T(8,128)(2,1)S(1)} collective-permute-done((bf16[4,48,768]{2,1,0:T(8,128)(2,1)S(1)}, bf16[4,48,768]{2,1,0:T(8,128)(2,1)S(1)}, u32[]{:S(2)}, u32[]{:S(2)}) %collective-permute-start.11) | collective-permute-done | bytes 294944 | tf_op jit(solution)/shard_map/ppermute | solution.py:468
  78.2 0.9 maximum_select_fusion.1
  79.0 1.1 maximum_select_fusion
  80.2 0.8 copy-done.17
  81.0 27.7 %shard_map.256 = (f32[1024,768]{1,0:T(8,128)}, bf16[1024,768]{1,0:T(8,128)(2,1)}, bf16[1024,768]{1,0:T(8,128)(2,1)}, bf16[2,4,96,768]{3,2,1,0:T(8,128)(2,1)}, bf...) custom-call(s32[7]{0:T(128)} %stack.100.refs_0_.info_ref, ...), custom_call_target="tpu_custom_call" | custom-call | flops 28000000000 | bytes 84000000 | tf_op jit(solution)/shard_map/pallas_call | solution.py:597
  109.3 1.5 collective-permute-start.24
  110.8 1.6 collective-permute-start.25
  112.4 2.4 collective-permute-done.16.refs_2_
  114.8 25.2 %shard_map.258 = (f32[1024,768]{1,0:T(8,128)}, bf16[1024,768]{1,0:T(8,128)(2,1)}, bf16[768,1024]{1,0:T(8,128)(2,1)}, f32[1024,768]{1,0:T(8,128)}, bf16[4,96,768]...) custom-call(s32[7]{0:T(128)} %stack.100.refs_0_.info_ref, ...), custom_call_target="tpu_custom_call" | custom-call | flops 20999999488 | bytes 63000000 | tf_op jit(solution)/shard_map/pallas_call | solution.py:653
  140.0 1.6 collective-permute-start.27
  141.5 1.0 copy-done.6
  142.5 19.6 %shard_map.259 = (bf16[1024,768]{1,0:T(8,128)(2,1)}, bf16[4,96,768]{2,1,0:T(8,128)(2,1)}, bf16[4,96,768]{2,1,0:T(8,128)(2,1)}, f32[1,576]{1,0:T(1,128)}) custom-call(s32[7]{0:T(128)} %stack.100.refs_0_.info_ref, bf16[1024,768]{1,0:T(8,128)(2,1)} %get-tuple-element.92.refs_1_, f32[1024,768]{1,0:T(8,128)} %get-tuple-element.93.refs_2_, ...), custom_call_target="tpu_custom_call" | custom-call | flops 16999999488 | bytes 51000000 | tf_op jit(solution)/shard_map/pallas_call | solution.py:669
  162.5 1.4 copy-done
  163.9 0.9 fusion.3
  164.8 1.7 collective-permute-start.32
  166.5 3.5 %shard_map.257 = bf16[512,768]{1,0:T(8,128)(2,1)} custom-call(s32[7]{0:T(128)} %stack.100.refs_0_.info_ref, f32[1024,768]{1,0:T(8,128)} %get-tuple-element.82.residual_ref.refs_3_, bf16[1024,768]{1,0:T(8,128)(2,1)} %get-tuple-element.83.mlp_a_ref.refs_6_, bf16[1024,768]{1,0:T(8,128)(2,1)} %copy-done.14, f32[768]{0:T(1024)} %refs_8_.1), custom_call_target="tpu_custom_call" | custom-call | flops 3000000000 | bytes 9000000 | tf_op jit(solution)/shard_map/pallas_call | solution.py:620
  170.4 1.6 convert_add_fusion.1
  172.1 1.6 collective-permute-start.26
  174.2 1.2 add_convert_fusion
  175.5 5.8 %collective-permute-done.32 = bf16[4,96,768]{2,1,0:T(8,128)(2,1)} collective-permute-done((bf16[4,96,768]{2,1,0:T(8,128)(2,1)}, bf16[4,96,768]{2,1,0:T(8,128)(2,1)}, u32[]{:S(2)}, u32[]{:S(2)}) %collective-permute-start.32) | collective-permute-done | bytes 589856 | tf_op jit(solution)/shard_map/ppermute | solution.py:468
  181.3 1.7 collective-permute-start.28
  183.0 1.2 fusion.1
  184.2 1.0 copy-done.2
  185.9 12.2 %collective-permute-done.14.near_ref = bf16[512,768]{1,0:T(8,128)(2,1)} collective-permute-done((bf16[512,768]{1,0:T(8,128)(2,1)}, bf16[512,768]{1,0:T(8,128)(2,1)}, u32[]{:S(2)}, u32[]{:S(2)}) %collective-permute-start.14) | collective-permute-done | bytes 786464 | tf_op jit(solution)/shard_map/ppermute | solution.py:468
  198.2 7.6 %shard_map.260 = (f32[2048,768]{1,0:T(8,128)}, bf16[512,768]{1,0:T(8,128)(2,1)}, f32[8,768]{1,0:T(8,128)}, f32[8,768]{1,0:T(8,128)}) custom-call(s32[7]{0:T(128)} %stack.100.refs_0_.info_ref, bf16[2048,768]{1,0:T(8,128)(2,1)} %x_ref.1, bf16[1024,768]{1,0:T(8,128)(2,1)} %get-tuple-element.100.grad_a_ref, ...), custom_call_target="tpu_custom_call" | custom-call | flops 7000000000 | bytes 21000000 | tf_op jit(solution)/shard_map/pallas_call | solution.py:683
  205.8 5.0 %collective-permute-done.26 = bf16[2,192,768]{2,1,0:T(8,128)(2,1)} collective-permute-done((bf16[2,192,768]{2,1,0:T(8,128)(2,1)S(1)}, bf16[2,192,768]{2,1,0:T(8,128)(2,1)}, u32[]{:S(2)}, u32[]{:S(2)}) %collective-permute-start.26) | collective-permute-done | bytes 589856 | tf_op jit(solution)/shard_map/ppermute | solution.py:468
  210.8 1.7 collective-permute-start.18
  212.5 10.9 %collective-permute-done.28 = bf16[4,96,768]{2,1,0:T(8,128)(2,1)} collective-permute-done((bf16[4,96,768]{2,1,0:T(8,128)(2,1)S(1)}, bf16[4,96,768]{2,1,0:T(8,128)(2,1)}, u32[]{:S(2)}, u32[]{:S(2)}) %collective-permute-start.28) | collective-permute-done | bytes 589856 | tf_op jit(solution)/shard_map/ppermute | solution.py:468
  223.4 1.2 fusion
  225.3 1.7 collective-permute-start.20
  227.0 1.0 bitcast_add_fusion.1
  228.7 11.6 %collective-permute-done.20 = f32[8,768]{1,0:T(8,128)S(1)} collective-permute-done((f32[8,768]{1,0:T(8,128)S(1)}, f32[8,768]{1,0:T(8,128)S(1)}, u32[]{:S(2)}, u32[]{:S(2)}) %collective-permute-start.20) | collective-permute-done | bytes 24608 | tf_op jit(solution)/shard_map/ppermute | solution.py:468
  240.8 1.4 convert_add_fusion.2
  242.3 1.9 collective-permute-done.21
  244.2 2.1 collective-permute-start.30
  246.3 2.0 collective-permute-done.22
  248.2 0.9 collective-permute-start.23
  249.1 4.5 %shard_map.261 = bf16[2048,768]{1,0:T(8,128)(2,1)} custom-call(s32[7]{0:T(128)} %stack.100.refs_0_.info_ref, bf16[512,768]{1,0:T(8,128)(2,1)} %collective-permute-done.14.near_ref, bf16[512,768]{1,0:T(8,128)(2,1)} %collective-permute-done.15.far_ref, bf16[2048,768]{1,0:T(8,128)(2,1)} %get-tuple-element.110.whole_ref), custom_call_target="tpu_custom_call", output_to_operand_aliasing={{}: (3, {})} | custom-call | flops 3000000000 | bytes 9000000 | tf_op jit(solution)/shard_map/pallas_call | solution.py:710
  255.1 1.4 reshape.312
  257.1 1.3 fusion.12
  258.4 1.7 bitcast_add_fusion.4
  260.1 1.0 bitcast_add_fusion.2
  261.1 2.1 collective-permute-start.31
  263.2 1.0 bitcast_add_fusion
  264.3 0.9 collective-permute-start.36
  265.2 6.8 %collective-permute-done.31 = bf16[96,768]{1,0:T(8,128)(2,1)S(1)} collective-permute-done((bf16[96,768]{1,0:T(8,128)(2,1)S(1)}, bf16[96,768]{1,0:T(8,128)(2,1)S(1)}, u32[]{:S(2)}, u32[]{:S(2)}) %collective-permute-start.31) | collective-permute-done | bytes 147488 | tf_op jit(solution)/shard_map/ppermute | solution.py:468
  272.1 0.9 copy.40
  273.7 1.4 collective-permute-done.36
  275.9 0.9 copy-done.7
  276.8 4.8 %shard_map.262 = f32[2048,768]{1,0:T(8,128)} custom-call(s32[7]{0:T(128)} %stack.100.refs_0_.info_ref, bf16[512,768]{1,0:T(8,128)(2,1)} %collective-permute-done.18.near_ref, bf16[512,768]{1,0:T(8,128)(2,1)} %copy-done.7, f32[2048,768]{1,0:T(8,128)} %get-tuple-element.111.whole_ref), custom_call_target="tpu_custom_call", output_to_operand_aliasing={{}: (3, {})} | custom-call | flops 3000000000 | bytes 9000000 | tf_op jit(solution)/shard_map/pallas_call | solution.py:710
  (115 shorter events, 13.5 us)
Async XLA Ops:
  1.6 4.6 %copy-start.13 = (f32[2,3,64]{2,0,1:T(2,128)S(1)}, f32[2,3,64]{2,0,1:T(2,128)}, u32[]{:S(2)}) copy-start(f32[2,3,64]{2,0,1:T(2,128)} %param.20) | copy-start | bytes 4612
  1.6 4.7 %copy-start.12 = (f32[6,128]{1,0:T(8,128)S(1)}, f32[6,128]{1,0:T(8,128)}, u32[]{:S(2)}) copy-start(f32[6,128]{1,0:T(8,128)} %param.26) | copy-start | bytes 9220
  1.6 12.1 %copy-start.15 = (bf16[768,3,3,64]{0,3,2,1:T(8,128)(2,1)S(1)}, bf16[768,3,3,64]{0,3,2,1:T(8,128)(2,1)}, u32[]{:S(2)}) copy-start(bf16[768,3,3,64]{0,3,2,1:T(8,128)(2,1)} %param.19) | copy-start | bytes 2654212
  1.6 7.2 %collective-permute-start = (bf16[1,96,768]{2,1,0:T(8,128)(2,1)S(1)}, bf16[1,96,768]{2,1,0:T(8,128)(2,1)S(1)}, u32[]{:S(2)}, u32[]{:S(2)}) collective-permute-start(bf16[1,96,768]{2,1,0:T(8,128)(2,1)S(1)} %dynamic-slice_bitcast_fusion), channel_id=1, source_target_pairs={{0,2},{1,3},{2,0},{3,1},{4,6},{5,7},{6,4},{7,5},{8,10},{9,11},{10,... | collective-permute-start | bytes 442376 | tf_op jit(solution)/shard_map/ppermute | solution.py:468
  6.0 10.3 %collective-permute-start.2 = (bf16[1,48,768]{2,1,0:T(8,128)(2,1)S(1)}, bf16[1,48,768]{2,1,0:T(8,128)(2,1)S(1)}, u32[]{:S(2)}, u32[]{:S(2)}) collective-permute-start(bf16[1,48,768]{2,1,0:T(8,128)(2,1)S(1)} %dynamic-slice_bitcast_fusion.1), channel_id=1, source_target_pairs={{0,2},{1,3},{2,0},{3,1},{4,6},{5,7},{6,4},{7,5},{8,10},{9,11},{10,... | collective-permute-start | bytes 221192 | tf_op jit(solution)/shard_map/ppermute | solution.py:468
  8.8 12.8 %collective-permute-start.1 = (bf16[1,96,768]{2,1,0:T(8,128)(2,1)S(1)}, bf16[1,96,768]{2,1,0:T(8,128)(2,1)S(1)}, u32[]{:S(2)}, u32[]{:S(2)}) collective-permute-start(bf16[1,96,768]{2,1,0:T(8,128)(2,1)S(1)} %collective-permute-done), channel_id=1, source_target_pairs={{0,16},{4,20},{8,24},{12,28},{16,0},{20,4},{24,8},{28,12},{1,17},{... | collective-permute-start | bytes 442376 | tf_op jit(solution)/shard_map/ppermute | solution.py:468
  11.8 27.0 %collective-permute-start.7 = (f32[1,1152]{1,0:T(1,128)S(1)}, f32[1,1152]{1,0:T(1,128)S(1)}, u32[]{:S(2)}, u32[]{:S(2)}) collective-permute-start(f32[1,1152]{1,0:T(1,128)S(1)} %pad_maximum_fusion.1), channel_id=1, source_target_pairs={{0,2},{1,3},{2,0},{3,1},{4,6},{5,7},{6,4},{7,5},{8,10},{9,11},{10,... | collective-permute-start | bytes 13832 | tf_op jit(solution)/shard_map/ppermute | solution.py:468
  13.7 25.9 %collective-permute-start.4 = (bf16[576,768]{1,0:T(8,128)(2,1)S(1)}, bf16[576,768]{1,0:T(8,128)(2,1)S(1)}, u32[]{:S(2)}, u32[]{:S(2)}) collective-permute-start(bf16[576,768]{1,0:T(8,128)(2,1)S(1)} %bitcast.134), channel_id=1, source_target_pairs={{0,2},{1,3},{2,0},{3,1},{4,6},{5,7},{6,4},{7,5},{8,10},{9,11},{10,... | collective-permute-start | bytes 2654216 | tf_op jit(solution)/shard_map/ppermute | solution.py:468
  13.9 25.7 %collective-permute-start.8 = (bf16[192,768]{1,0:T(8,128)(2,1)}, bf16[192,768]{1,0:T(8,128)(2,1)}, u32[]{:S(2)}, u32[]{:S(2)}) collective-permute-start(bf16[192,768]{1,0:T(8,128)(2,1)} %bitcast.135), channel_id=1, source_target_pairs={{0,2},{1,3},{2,0},{3,1},{4,6},{5,7},{6,4},{7,5},{8,10},{9,11},{10,... | collective-permute-start | bytes 884744 | tf_op jit(solution)/shard_map/ppermute | solution.py:468
  16.3 5.3 %collective-permute-start.3 = (bf16[1,48,768]{2,1,0:T(8,128)(2,1)S(1)}, bf16[1,48,768]{2,1,0:T(8,128)(2,1)S(1)}, u32[]{:S(2)}, u32[]{:S(2)}) collective-permute-start(bf16[1,48,768]{2,1,0:T(8,128)(2,1)S(1)} %collective-permute-done.2), channel_id=1, source_target_pairs={{0,16},{4,20},{8,24},{12,28},{16,0},{20,4},{24,8},{28,12},{1,17},{... | collective-permute-start | bytes 221192 | tf_op jit(solution)/shard_map/ppermute | solution.py:468
  21.6 17.2 %collective-permute-start.6 = (bf16[2,48,768]{2,1,0:T(8,128)(2,1)S(1)}, bf16[2,48,768]{2,1,0:T(8,128)(2,1)S(1)}, u32[]{:S(2)}, u32[]{:S(2)}) collective-permute-start(bf16[2,48,768]{2,1,0:T(8,128)(2,1)S(1)} %maximum_select_fusion.6), channel_id=1, source_target_pairs={{0,8},{4,12},{8,0},{12,4},{16,24},{20,28},{24,16},{28,20},{1,9},{5... | collective-permute-start | bytes 442376 | tf_op jit(solution)/shard_map/ppermute | solution.py:468
  23.3 15.6 %collective-permute-start.5 = (bf16[2,96,768]{2,1,0:T(8,128)(2,1)S(1)}, bf16[2,96,768]{2,1,0:T(8,128)(2,1)S(1)}, u32[]{:S(2)}, u32[]{:S(2)}) collective-permute-start(bf16[2,96,768]{2,1,0:T(8,128)(2,1)S(1)} %maximum_select_fusion.3), channel_id=1, source_target_pairs={{0,8},{4,12},{8,0},{12,4},{16,24},{20,28},{24,16},{28,20},{1,9},{5... | collective-permute-start | bytes 884744 | tf_op jit(solution)/shard_map/ppermute | solution.py:468
  39.6 0.9 copy-start.16
  55.9 24.3 %collective-permute-start.9 = (bf16[1024,768]{1,0:T(8,128)(2,1)}, bf16[1024,768]{1,0:T(8,128)(2,1)}, u32[]{:S(2)}, u32[]{:S(2)}) collective-permute-start(bf16[1024,768]{1,0:T(8,128)(2,1)} %get-tuple-element.79.branch_a_ref), channel_id=1, source_target_pairs={{0,1},{1,0},{2,3},{3,2},{4,5},{5,4},{6,7},{7,6},{8,9},{9,8},{10,11... | collective-permute-start | bytes 4718600 | tf_op jit(solution)/shard_map/ppermute | solution.py:468
  55.9 24.2 %collective-permute-start.10 = (bf16[384,768]{1,0:T(8,128)(2,1)S(1)}, bf16[384,768]{1,0:T(8,128)(2,1)S(1)}, u32[]{:S(2)}, u32[]{:S(2)}) collective-permute-start(bf16[384,768]{1,0:T(8,128)(2,1)S(1)} %get-tuple-element.146), channel_id=1, source_target_pairs={{0,2},{1,3},{2,0},{3,1},{4,6},{5,7},{6,4},{7,5},{8,10},{9,11},{10,... | collective-permute-start | bytes 1769480 | tf_op jit(solution)/shard_map/ppermute | solution.py:468
  56.4 22.7 %collective-permute-start.12 = (bf16[4,96,768]{2,1,0:T(8,128)(2,1)S(1)}, bf16[4,96,768]{2,1,0:T(8,128)(2,1)S(1)}, u32[]{:S(2)}, u32[]{:S(2)}) collective-permute-start(bf16[4,96,768]{2,1,0:T(8,128)(2,1)S(1)} %bitcast.111), channel_id=1, source_target_pairs={{0,4},{4,0},{8,12},{12,8},{16,20},{20,16},{24,28},{28,24},{1,5},{5... | collective-permute-start | bytes 1769480 | tf_op jit(solution)/shard_map/ppermute | solution.py:468
  58.0 20.2 %collective-permute-start.11 = (bf16[4,48,768]{2,1,0:T(8,128)(2,1)S(1)}, bf16[4,48,768]{2,1,0:T(8,128)(2,1)S(1)}, u32[]{:S(2)}, u32[]{:S(2)}) collective-permute-start(bf16[4,48,768]{2,1,0:T(8,128)(2,1)S(1)} %bitcast.114), channel_id=1, source_target_pairs={{0,4},{4,0},{8,12},{12,8},{16,20},{20,16},{24,28},{28,24},{1,5},{5... | collective-permute-start | bytes 884744 | tf_op jit(solution)/shard_map/ppermute | solution.py:468
  80.2 0.8 copy-start.17
  108.7 3.7 %collective-permute-start.13 = (bf16[1024,768]{1,0:T(8,128)(2,1)}, bf16[1024,768]{1,0:T(8,128)(2,1)S(1)}, u32[]{:S(2)}, u32[]{:S(2)}) collective-permute-start(bf16[1024,768]{1,0:T(8,128)(2,1)} %get-tuple-element.83.mlp_a_ref.refs_6_), channel_id=1, source_target_pairs={{0,1},{1,0},{2,3},{3,2},{4,5},{5,4},{6,7},{7,6},{8,9},{9,8},{10,11... | collective-permute-start | bytes 4718600 | tf_op jit(solution)/shard_map/ppermute | solution.py:468
  108.8 6.0 %collective-permute-start.16 = (bf16[1024,768]{1,0:T(8,128)(2,1)}, bf16[1024,768]{1,0:T(8,128)(2,1)}, u32[]{:S(2)}, u32[]{:S(2)}) collective-permute-start(bf16[1024,768]{1,0:T(8,128)(2,1)} %get-tuple-element.84.refs_1_), channel_id=1, source_target_pairs={{0,1},{1,0},{2,3},{3,2},{4,5},{5,4},{6,7},{7,6},{8,9},{9,8},{10,11... | collective-permute-start | bytes 4718600 | tf_op jit(solution)/shard_map/ppermute | solution.py:468
  109.3 32.2 %collective-permute-start.24 = (bf16[2,4,96,768]{3,2,1,0:T(8,128)(2,1)}, bf16[2,4,96,768]{3,2,1,0:T(8,128)(2,1)S(1)}, u32[]{:S(2)}, u32[]{:S(2)}) collective-permute-start(bf16[2,4,96,768]{3,2,1,0:T(8,128)(2,1)} %get-tuple-element.116), channel_id=1, source_target_pairs={{0,4},{4,0},{8,12},{12,8},{16,20},{20,16},{24,28},{28,24},{1,5},{5... | collective-permute-start | bytes 3538952 | tf_op jit(solution)/shard_map/ppermute | solution.py:468
  110.8 30.7 %collective-permute-start.25 = (bf16[2,2,192,768]{3,2,1,0:T(8,128)(2,1)}, bf16[2,2,192,768]{3,2,1,0:T(8,128)(2,1)S(1)}, u32[]{:S(2)}, u32[]{:S(2)}) collective-permute-start(bf16[2,2,192,768]{3,2,1,0:T(8,128)(2,1)} %get-tuple-element.117), channel_id=1, source_target_pairs={{0,8},{4,12},{8,0},{12,4},{16,24},{20,28},{24,16},{28,20},{1,9},{5... | collective-permute-start | bytes 3538952 | tf_op jit(solution)/shard_map/ppermute | solution.py:468
  112.4 2.4 copy-start.14
  140.0 33.8 %collective-permute-start.27 = (bf16[4,96,768]{2,1,0:T(8,128)(2,1)}, bf16[4,96,768]{2,1,0:T(8,128)(2,1)}, u32[]{:S(2)}, u32[]{:S(2)}) collective-permute-start(bf16[4,96,768]{2,1,0:T(8,128)(2,1)} %get-tuple-element.120), channel_id=1, source_target_pairs={{0,4},{4,0},{8,12},{12,8},{16,20},{20,16},{24,28},{28,24},{1,5},{5... | collective-permute-start | bytes 1769480 | tf_op jit(solution)/shard_map/ppermute | solution.py:468
  141.5 1.0 copy-start.6
  142.5 19.7 %copy-start.5 = (bf16[2,4,96,768]{3,2,1,0:T(8,128)(2,1)S(1)}, bf16[2,4,96,768]{3,2,1,0:T(8,128)(2,1)}, u32[]{:S(2)}) copy-start(bf16[2,4,96,768]{3,2,1,0:T(8,128)(2,1)} %get-tuple-element.126) | copy-start | bytes 3538948
  162.2 36.0 %collective-permute-start.17 = (bf16[1024,768]{1,0:T(8,128)(2,1)}, bf16[1024,768]{1,0:T(8,128)(2,1)}, u32[]{:S(2)}, u32[]{:S(2)}) collective-permute-start(bf16[1024,768]{1,0:T(8,128)(2,1)} %get-tuple-element.100.grad_a_ref), channel_id=1, source_target_pairs={{0,1},{1,0},{2,3},{3,2},{4,5},{5,4},{6,7},{7,6},{8,9},{9,8},{10,11... | collective-permute-start | bytes 4718600 | tf_op jit(solution)/shard_map/ppermute | solution.py:468
  162.5 1.4 copy-start
  164.8 5.6 %copy-start.4 = (bf16[2,2,192,768]{3,2,1,0:T(8,128)(2,1)S(1)}, bf16[2,2,192,768]{3,2,1,0:T(8,128)(2,1)}, u32[]{:S(2)}) copy-start(bf16[2,2,192,768]{3,2,1,0:T(8,128)(2,1)} %get-tuple-element.115) | copy-start | bytes 3538948
  164.8 16.5 %collective-permute-start.32 = (bf16[4,96,768]{2,1,0:T(8,128)(2,1)}, bf16[4,96,768]{2,1,0:T(8,128)(2,1)}, u32[]{:S(2)}, u32[]{:S(2)}) collective-permute-start(bf16[4,96,768]{2,1,0:T(8,128)(2,1)} %fusion.3), channel_id=1, source_target_pairs={{0,2},{1,3},{2,0},{3,1},{4,6},{5,7},{6,4},{7,5},{8,10},{9,11},{10,... | collective-permute-start | bytes 1769480 | tf_op jit(solution)/shard_map/ppermute | solution.py:468
  169.9 28.2 %collective-permute-start.14 = (bf16[512,768]{1,0:T(8,128)(2,1)}, bf16[512,768]{1,0:T(8,128)(2,1)}, u32[]{:S(2)}, u32[]{:S(2)}) collective-permute-start(bf16[512,768]{1,0:T(8,128)(2,1)} %shard_map.257), channel_id=1, source_target_pairs={{0,2},{1,3},{2,0},{3,1},{4,6},{5,7},{6,4},{7,5},{8,10},{9,11},{10,... | collective-permute-start | bytes 2359304 | tf_op jit(solution)/shard_map/ppermute | solution.py:468
  170.4 3.8 %copy-start.8 = (bf16[4,96,768]{2,1,0:T(8,128)(2,1)S(1)}, bf16[4,96,768]{2,1,0:T(8,128)(2,1)}, u32[]{:S(2)}) copy-start(bf16[4,96,768]{2,1,0:T(8,128)(2,1)} %get-tuple-element.119) | copy-start | bytes 1769476
  172.0 11.0 %copy-start.1 = (f32[2,4,96,768]{3,2,1,0:T(8,128)S(1)}, f32[2,4,96,768]{3,2,1,0:T(8,128)}, u32[]{:S(2)}) copy-start(f32[2,4,96,768]{3,2,1,0:T(8,128)} %copy-done) | copy-start | bytes 7077892
  172.1 38.7 %collective-permute-start.26 = (bf16[2,192,768]{2,1,0:T(8,128)(2,1)S(1)}, bf16[2,192,768]{2,1,0:T(8,128)(2,1)}, u32[]{:S(2)}, u32[]{:S(2)}) collective-permute-start(bf16[2,192,768]{2,1,0:T(8,128)(2,1)S(1)} %fusion.2), channel_id=1, source_target_pairs={{0,2},{1,3},{2,0},{3,1},{4,6},{5,7},{6,4},{7,5},{8,10},{9,11},{10,... | collective-permute-start | bytes 1769480 | tf_op jit(solution)/shard_map/ppermute | solution.py:468
  173.7 38.8 %collective-permute-start.29 = (bf16[4,96,768]{2,1,0:T(8,128)(2,1)}, bf16[4,96,768]{2,1,0:T(8,128)(2,1)}, u32[]{:S(2)}, u32[]{:S(2)}) collective-permute-start(bf16[4,96,768]{2,1,0:T(8,128)(2,1)} %get-tuple-element.122), channel_id=1, source_target_pairs={{0,4},{4,0},{8,12},{12,8},{16,20},{20,16},{24,28},{28,24},{1,5},{5... | collective-permute-start | bytes 1769480 | tf_op jit(solution)/shard_map/ppermute | solution.py:468
  181.3 42.1 %collective-permute-start.28 = (bf16[4,96,768]{2,1,0:T(8,128)(2,1)S(1)}, bf16[4,96,768]{2,1,0:T(8,128)(2,1)}, u32[]{:S(2)}, u32[]{:S(2)}) collective-permute-start(bf16[4,96,768]{2,1,0:T(8,128)(2,1)S(1)} %add_convert_fusion), channel_id=1, source_target_pairs={{0,2},{1,3},{2,0},{3,1},{4,6},{5,7},{6,4},{7,5},{8,10},{9,11},{10,... | collective-permute-start | bytes 1769480 | tf_op jit(solution)/shard_map/ppermute | solution.py:468
  184.2 1.0 copy-start.2
  198.2 27.1 %collective-permute-start.33 = (bf16[2,96,768]{2,1,0:T(8,128)(2,1)}, bf16[2,96,768]{2,1,0:T(8,128)(2,1)}, u32[]{:S(2)}, u32[]{:S(2)}) collective-permute-start(bf16[2,96,768]{2,1,0:T(8,128)(2,1)} %fusion.5), channel_id=1, source_target_pairs={{0,8},{4,12},{8,0},{12,4},{16,24},{20,28},{24,16},{28,20},{1,9},{5... | collective-permute-start | bytes 884744 | tf_op jit(solution)/shard_map/ppermute | solution.py:468
  198.2 46.0 %collective-permute-start.15 = (bf16[512,768]{1,0:T(8,128)(2,1)}, bf16[512,768]{1,0:T(8,128)(2,1)}, u32[]{:S(2)}, u32[]{:S(2)}) collective-permute-start(bf16[512,768]{1,0:T(8,128)(2,1)} %collective-permute-done.14.near_ref), channel_id=1, source_target_pairs={{0,1},{1,0},{2,3},{3,2},{4,5},{5,4},{6,7},{7,6},{8,9},{9,8},{10,11... | collective-permute-start | bytes 2359304 | tf_op jit(solution)/shard_map/ppermute | solution.py:468
  210.8 14.5 %copy-start.18 = (f32[8,768]{1,0:T(8,128)S(1)}, f32[8,768]{1,0:T(8,128)}, u32[]{:S(2)}) copy-start(f32[8,768]{1,0:T(8,128)} %get-tuple-element.113) | copy-start | bytes 73732
  210.8 16.2 %copy-start.3 = (f32[4,96,768]{2,1,0:T(8,128)S(1)}, f32[4,96,768]{2,1,0:T(8,128)}, u32[]{:S(2)}) copy-start(f32[4,96,768]{2,1,0:T(8,128)} %copy-done.2) | copy-start | bytes 3538948
  210.8 52.4 %collective-permute-start.18 = (bf16[512,768]{1,0:T(8,128)(2,1)}, bf16[512,768]{1,0:T(8,128)(2,1)}, u32[]{:S(2)}, u32[]{:S(2)}) collective-permute-start(bf16[512,768]{1,0:T(8,128)(2,1)} %get-tuple-element.107), channel_id=1, source_target_pairs={{0,2},{1,3},{2,0},{3,1},{4,6},{5,7},{6,4},{7,5},{8,10},{9,11},{10,... | collective-permute-start | bytes 2359304 | tf_op jit(solution)/shard_map/ppermute | solution.py:468
  224.6 15.6 %copy-start.11 = (f32[8,768]{1,0:T(8,128)S(1)}, f32[8,768]{1,0:T(8,128)}, u32[]{:S(2)}) copy-start(f32[8,768]{1,0:T(8,128)} %get-tuple-element.112) | copy-start | bytes 73732
  224.6 16.2 %copy-start.9 = (bf16[4,96,768]{2,1,0:T(8,128)(2,1)S(1)}, bf16[4,96,768]{2,1,0:T(8,128)(2,1)}, u32[]{:S(2)}) copy-start(bf16[4,96,768]{2,1,0:T(8,128)(2,1)} %get-tuple-element.114) | copy-start | bytes 1769476
  224.7 35.4 %collective-permute-start.35 = (bf16[2,96,768]{2,1,0:T(8,128)(2,1)S(1)}, bf16[2,96,768]{2,1,0:T(8,128)(2,1)}, u32[]{:S(2)}, u32[]{:S(2)}) collective-permute-start(bf16[2,96,768]{2,1,0:T(8,128)(2,1)S(1)} %fusion.6), channel_id=1, source_target_pairs={{0,4},{4,0},{8,12},{12,8},{16,20},{20,16},{24,28},{28,24},{1,5},{5... | collective-permute-start | bytes 884744 | tf_op jit(solution)/shard_map/ppermute | solution.py:468
  225.3 15.0 %collective-permute-start.20 = (f32[8,768]{1,0:T(8,128)S(1)}, f32[8,768]{1,0:T(8,128)S(1)}, u32[]{:S(2)}, u32[]{:S(2)}) collective-permute-start(f32[8,768]{1,0:T(8,128)S(1)} %copy-done.18), channel_id=1, source_target_pairs={{0,2},{1,3},{2,0},{3,1},{4,6},{5,7},{6,4},{7,5},{8,10},{9,11},{10,... | collective-permute-start | bytes 73736 | tf_op jit(solution)/shard_map/ppermute | solution.py:468
  228.7 29.7 %collective-permute-start.34 = (bf16[96,768]{1,0:T(8,128)(2,1)}, bf16[96,768]{1,0:T(8,128)(2,1)}, u32[]{:S(2)}, u32[]{:S(2)}) collective-permute-start(bf16[96,768]{1,0:T(8,128)(2,1)} %fusion.10), channel_id=1, source_target_pairs={{0,16},{4,20},{8,24},{12,28},{16,0},{20,4},{24,8},{28,12},{1,17},{... | collective-permute-start | bytes 442376 | tf_op jit(solution)/shard_map/ppermute | solution.py:468
  240.2 3.9 %collective-permute-start.21 = (f32[8,768]{1,0:T(8,128)S(1)}, f32[8,768]{1,0:T(8,128)S(1)}, u32[]{:S(2)}, u32[]{:S(2)}) collective-permute-start(f32[8,768]{1,0:T(8,128)S(1)} %add.104), channel_id=1, source_target_pairs={{0,4},{4,0},{8,12},{12,8},{16,20},{20,16},{24,28},{28,24},{1,5},{5... | collective-permute-start | bytes 73736 | tf_op jit(solution)/shard_map/ppermute | solution.py:468
  244.1 4.1 %collective-permute-start.22 = (f32[8,768]{1,0:T(8,128)S(1)}, f32[8,768]{1,0:T(8,128)S(1)}, u32[]{:S(2)}, u32[]{:S(2)}) collective-permute-start(f32[8,768]{1,0:T(8,128)S(1)} %add.105), channel_id=1, source_target_pairs={{0,8},{4,12},{8,0},{12,4},{16,24},{20,28},{24,16},{28,20},{1,9},{5... | collective-permute-start | bytes 73736 | tf_op jit(solution)/shard_map/ppermute | solution.py:468
  244.2 15.9 %collective-permute-start.30 = (bf16[2,96,768]{2,1,0:T(8,128)(2,1)S(1)}, bf16[2,96,768]{2,1,0:T(8,128)(2,1)}, u32[]{:S(2)}, u32[]{:S(2)}) collective-permute-start(bf16[2,96,768]{2,1,0:T(8,128)(2,1)S(1)} %fusion.4), channel_id=1, source_target_pairs={{0,8},{4,12},{8,0},{12,4},{16,24},{20,28},{24,16},{28,20},{1,9},{5... | collective-permute-start | bytes 884744 | tf_op jit(solution)/shard_map/ppermute | solution.py:468
  248.2 5.4 %collective-permute-start.23 = (f32[8,768]{1,0:T(8,128)S(1)}, f32[8,768]{1,0:T(8,128)S(1)}, u32[]{:S(2)}, u32[]{:S(2)}) collective-permute-start(f32[8,768]{1,0:T(8,128)S(1)} %add.106), channel_id=1, source_target_pairs={{0,16},{4,20},{8,24},{12,28},{16,0},{20,4},{24,8},{28,12},{1,17},{... | collective-permute-start | bytes 73736 | tf_op jit(solution)/shard_map/ppermute | solution.py:468
  253.6 0.6 copy-start.10
  261.1 10.9 %collective-permute-start.31 = (bf16[96,768]{1,0:T(8,128)(2,1)S(1)}, bf16[96,768]{1,0:T(8,128)(2,1)S(1)}, u32[]{:S(2)}, u32[]{:S(2)}) collective-permute-start(bf16[96,768]{1,0:T(8,128)(2,1)S(1)} %fusion.9), channel_id=1, source_target_pairs={{0,16},{4,20},{8,24},{12,28},{16,0},{20,4},{24,8},{28,12},{1,17},{... | collective-permute-start | bytes 442376 | tf_op jit(solution)/shard_map/ppermute | solution.py:468
  263.2 12.6 %collective-permute-start.19 = (bf16[512,768]{1,0:T(8,128)(2,1)}, bf16[512,768]{1,0:T(8,128)(2,1)S(1)}, u32[]{:S(2)}, u32[]{:S(2)}) collective-permute-start(bf16[512,768]{1,0:T(8,128)(2,1)} %collective-permute-done.18.near_ref), channel_id=1, source_target_pairs={{0,1},{1,0},{2,3},{3,2},{4,5},{5,4},{6,7},{7,6},{8,9},{9,8},{10,11... | collective-permute-start | bytes 2359304 | tf_op jit(solution)/shard_map/ppermute | solution.py:468
  264.3 10.8 %collective-permute-start.36 = (bf16[96,768]{1,0:T(8,128)(2,1)S(1)}, bf16[96,768]{1,0:T(8,128)(2,1)S(1)}, u32[]{:S(2)}, u32[]{:S(2)}) collective-permute-start(bf16[96,768]{1,0:T(8,128)(2,1)S(1)} %fusion.11), channel_id=1, source_target_pairs={{0,16},{4,20},{8,24},{12,28},{16,0},{20,4},{24,8},{28,12},{1,17},{... | collective-permute-start | bytes 442376 | tf_op jit(solution)/shard_map/ppermute | solution.py:468
  275.9 0.9 copy-start.7
where the time goes:
time: 282 us
  Pallas kernels  123 us (44%)
  waiting for transfers between devices  83.2 us (30%)
  starting transfers between devices  36.9 us (13%)
  local copies, waits for them, and re-layouts  20.6 us (7%)
  other arithmetic  15.1 us (5%)
    ppermute x37, waiting for transfers between devices, exchange(): return lax.ppermute(value, axis_name, [(i, i ^ bit) for i in range(size)])  83.2 us
    ppermute x37, starting transfers between devices, exchange(): return lax.ppermute(value, axis_name, [(i, i ^ bit) for i in range(size)])  36.9 us
    pallas_call x1, Pallas kernels, body(): call(mlp_kernel, blocks, [row_spec(QUERY_ROWS, width, True), first_spec,...  27.7 us
    pallas_call x1, Pallas kernels, body(): call(backward_other, blocks, [back_rows, back_rows, back_rows, back_spec(...  25.2 us
    pallas_call x1, Pallas kernels, body(): call(backward_own, blocks, [back_rows, back_rows] + back_mix + [in_place,...  19.6 us
    pallas_call x1, Pallas kernels, body(): call(forward_other, blocks, [first_spec, whole((3 * local, width)), whole...  15.4 us
    pallas_call x1, Pallas kernels, body(): call(forward_own, blocks, [row_spec(QUERY_ROWS, width, True), whole((widt...  15 us
    add x9, other arithmetic, add(): return kept.astype(F32) + received.astype(F32)  10.3 us
  transfers between devices with their start and end apart: 37, of which 13 were waited for; matrix products, arithmetic and copies ran while one was open for 10% of the time, Pallas kernels for 27%

commit v1 on v0

--- a/solution.py
+++ b/solution.py
@@ -15,6 +15,8 @@
 BF16 = jnp.bfloat16
 F32 = jnp.float32
 VMEM_BYTES = 60 * 1024 * 1024
+DP = "dp"
+TENSOR = "tensor"
 
 
 def dot_nn(left, right):
@@ -418,6 +420,10 @@
     out_ref[...] = block_value(residual_ref, mlp_a_ref, mlp_b_ref, bias_ref)
 
 
+def fill_kernel(info_ref, come_ref, whole_ref, out_ref):
+    out_ref[...] = come_ref[...].astype(out_ref.dtype)
+
+
 def fill_both_kernel(info_ref, near_ref, far_ref, whole_ref, out_ref):
     from_near = (pl.program_id(0) * near_ref.shape[0]) // info_ref[4] == info_ref[2]
     out_ref[...] = jnp.where(from_near, near_ref[...], far_ref[...]).astype(out_ref.dtype)
@@ -482,9 +488,9 @@
         rows = row_count // 2
         blocks = rows // QUERY_ROWS
         half = rows // 2
-        place = lax.axis_index("tensor")
+        place = lax.axis_index(TENSOR)
         bits = dp_size.bit_length() - 1
-        position = lax.axis_index("dp")
+        position = lax.axis_index(DP)
         share = width // dp_size
         first_bit = next(bit for bit in range(bits) if (share << bit) % 16 == 0)
         second_bit = min(first_bit + 1, bits - 1)
@@ -497,10 +503,10 @@
         ).astype(jnp.int32)
 
         def core_swap(value):
-            return exchange(value, "tensor", tensor_size, 1)
+            return exchange(value, TENSOR, tensor_size, 1)
 
         def pair_swap(value):
-            return exchange(value, "tensor", tensor_size, 2)
+            return exchange(value, TENSOR, tensor_size, 2)
 
         qkv_own = w_qkv.transpose(1, 2, 3, 0).reshape(3 * local, width)
         out_own = w_out.reshape(local, width)
@@ -523,7 +529,7 @@
             )
 
         def dp_swap(values, bit):
-            return tuple(exchange(value, "dp", dp_size, 1 << bit) for value in values)
+            return tuple(exchange(value, DP, dp_size, 1 << bit) for value in values)
 
         parts = tuple(
             pair_swap(my_piece(matrix)) for matrix in (w_proj, w_fc[width // 2 :])
@@ -722,7 +728,25 @@
         block_near, block_far = after((block_near, block_far), grad_half)
         block_out = fill_both(block_out, block_near, block_far)
         grad_far = core_swap(grad_near)
-        grad_in = fill_both(grad_in, grad_near, grad_far)
+
+        def fill(target, come, part):
+            def index(step, info):
+                first = jnp.where(part == 0, info[2], 1 - info[2]) * quarter
+                return info[3] + first + step, 0
+
+            return call(
+                fill_kernel,
+                quarter,
+                [first_spec, pl.BlockSpec(memory_space=pl.ANY)],
+                pl.BlockSpec((QUERY_ROWS, width), index),
+                struct(target.shape, target.dtype),
+                [],
+                2,
+                {2: 0},
+            )(info, come, target)
+
+        grad_in = fill(grad_in, grad_near, 0)
+        grad_in = fill(grad_in, grad_far, 1)
 
         def pick(value, axis, which):
             return lax.dynamic_index_in_dim(value, which, axis, keepdims=False)
@@ -741,33 +765,35 @@
                 above = len([b for b in left[number:] if b > bit])
                 mine = (position >> bit) & 1
                 received = exchange(
-                    pick(value, above, 1 - mine).astype(BF16), "dp", dp_size, 1 << bit
+                    pick(value, above, 1 - mine).astype(BF16), DP, dp_size, 1 << bit
                 )
                 if number == 0:
                     received = after(received, grad_half)
                 value = add(pick(value, above, mine), received)
             return value
 
-        got_fc = exchange(fc_sent, "dp", dp_size, 1 << first_bit)
-        got_proj = exchange(proj_sent, "dp", dp_size, 1 << second_bit)
-        got_far = exchange(far_sent, "dp", dp_size, 1 << first_bit)
+        got_fc = exchange(fc_sent, DP, dp_size, 1 << first_bit)
+        got_proj = exchange(proj_sent, DP, dp_size, 1 << second_bit)
+        got_far = exchange(far_sent, DP, dp_size, 1 << first_bit)
         got_fc, got_proj = after((got_fc, got_proj), grad_branch)
-        half_fc = add(fc_kept, got_fc)
-        half_proj = add(proj_kept, got_proj)
-        come_fc = pair_swap(half_fc[1].astype(BF16))
-        come_proj = pair_swap(half_proj[1].astype(BF16))
-        got_near = exchange(near_sent, "dp", dp_size, 1 << first_bit)
+        half_fc = add(fc_kept[1], got_fc[1])
+        half_proj = add(proj_kept[1], got_proj[1])
+        come_fc = pair_swap(half_fc.astype(BF16))
+        come_proj = pair_swap(half_proj.astype(BF16))
+        got_near = exchange(near_sent, DP, dp_size, 1 << first_bit)
         got_far = after(got_far, grad_first)
         come_far = pair_swap(add(far_kept, got_far).astype(BF16))
-        come_fc = after(come_fc, grad_first)
-        come_proj, come_far, got_near = after((come_proj, come_far, got_near), grad_half)
-        fc_share = stages(parted(add(half_fc[0], come_fc)), others(first_bit))
-        proj_share = stages(parted(add(half_proj[0], come_proj)), others(second_bit))
+        come_fc, got_fc = after((come_fc, got_fc), grad_first)
+        come_proj, got_proj, come_far, got_near = after(
+            (come_proj, got_proj, come_far, got_near), grad_half
+        )
+        fc_share = stages(parted(add(add(fc_kept[0], got_fc[0]), come_fc)), others(first_bit))
+        proj_share = stages(parted(add(add(proj_kept[0], got_proj[0]), come_proj)), others(second_bit))
         att_half = parted(add(add(near_kept, got_near), come_far))
         att_share = stages(att_half, others(first_bit))
         small = small + small_come
         for bit in range(bits):
-            small_come = exchange(small, "dp", dp_size, 1 << bit)
+            small_come = exchange(small, DP, dp_size, 1 << bit)
             small = small + small_come
         shares = lax.dynamic_index_in_dim(
             small[0:6].reshape(6, dp_size, share), position, 1, keepdims=False
@@ -796,38 +822,38 @@
 
 def solution(mesh):
     in_specs = (
-        P("dp", None),
-        P("dp"),
+        P(DP, None),
+        P(DP),
         P(),
         P(),
-        P(None, None, "tensor", None),
-        P(None, "tensor", None),
-        P("tensor", None, None),
+        P(None, None, TENSOR, None),
+        P(None, TENSOR, None),
+        P(TENSOR, None, None),
         P(),
         P(),
         P(),
-        P(None, "tensor"),
-        P("tensor", None),
-        P("tensor", None),
+        P(None, TENSOR),
+        P(TENSOR, None),
+        P(TENSOR, None),
         P(),
-        P("dp", None),
+        P(DP, None),
     )
     out_specs = (
-        P("dp", None),
-        P("dp", None),
-        P("dp"),
-        P("dp"),
-        P("dp", None, "tensor", None),
-        P(None, "tensor", "dp"),
-        P("tensor", None, "dp"),
-        P("dp"),
-        P("dp"),
-        P("dp"),
-        P("dp", "tensor"),
-        P("tensor", "dp"),
-        P("tensor", "dp"),
-        P("dp"),
-    )
-    inner = make_body(mesh.shape["dp"], mesh.shape["tensor"])
+        P(DP, None),
+        P(DP, None),
+        P(DP),
+        P(DP),
+        P(DP, None, TENSOR, None),
+        P(None, TENSOR, DP),
+        P(TENSOR, None, DP),
+        P(DP),
+        P(DP),
+        P(DP),
+        P(DP, TENSOR),
+        P(TENSOR, DP),
+        P(TENSOR, DP),
+        P(DP),
+    )
+    inner = make_body(mesh.shape[DP], mesh.shape[TENSOR])
 
     return jax.shard_map(inner, mesh=mesh, in_specs=in_specs, out_specs=out_specs, check_vma=False)

time: 282 us -> 281 us (level)
  waiting for transfers between devices: 83.2 us -> 80.1 us
  starting transfers between devices: 36.9 us -> 40 us
    pallas_call x0 -> x2, Pallas kernels: none -> 5.72 us  [fill(): call(fill_kernel, quarter, [first_spec, pl.BlockSpec(memory_space=pl.ANY)...]
    pallas_call x2 -> x1, Pallas kernels: 9.27 us -> 4.51 us  [fill_both(): call(fill_both_kernel, blocks, [quarter_spec(0), quarter_spec(1), pl.Bloc...]
    unnamed x41, local copies, waits for them, and re-layouts: 7.3 us -> 3.91 us
    ppermute x37, waiting for transfers between devices: 83.2 us -> 80.1 us  [exchange(): return lax.ppermute(value, axis_name, [(i, i ^ bit) for i in range(size)])]
    ppermute x37, starting transfers between devices: 36.9 us -> 40 us  [exchange(): return lax.ppermute(value, axis_name, [(i, i ^ bit) for i in range(size)])]
    add x9 -> x7, other arithmetic: 10.3 us -> 7.68 us  [add(): return kept.astype(F32) + received.astype(F32)]
  transfers between devices with their start and end apart: 37 -> 37, of which waited for: 13 -> 15; matrix products, arithmetic and copies ran while one was open for 10% -> 11% of each run, Pallas kernels for 27% -> 28%
where the time goes in v1:
time: 281 us; the launch traced here: 280 us
  Pallas kernels  124 us (44%)
  waiting for transfers between devices  80.1 us (29%)
  starting transfers between devices  40 us (14%)
  local copies, waits for them, and re-layouts  18.5 us (7%)
  other arithmetic  15.2 us (5%)
    ppermute x37, waiting for transfers between devices, exchange(): return lax.ppermute(value, axis_name, [(i, i ^ bit) for i in range(size)])  80.1 us
    ppermute x37, starting transfers between devices, exchange(): return lax.ppermute(value, axis_name, [(i, i ^ bit) for i in range(size)])  40 us
    pallas_call x1, Pallas kernels, body(): call(mlp_kernel, blocks, [row_spec(QUERY_ROWS, width, True), first_spec,...  27.7 us
    pallas_call x1, Pallas kernels, body(): call(backward_other, blocks, [back_rows, back_rows, back_rows, back_spec(...  25.1 us
    pallas_call x1, Pallas kernels, body(): call(backward_own, blocks, [back_rows, back_rows] + back_mix + [in_place,...  19.6 us
    pallas_call x1, Pallas kernels, body(): call(forward_other, blocks, [first_spec, whole((3 * local, width)), whole...  15.4 us
    pallas_call x1, Pallas kernels, body(): call(forward_own, blocks, [row_spec(QUERY_ROWS, width, True), whole((widt...  15 us
    add x7, other arithmetic, add(): return kept.astype(F32) + received.astype(F32)  7.68 us
  transfers between devices with their start and end apart: 37, of which 15 were waited for; matrix products, arithmetic and copies ran while one was open for 11% of the time, Pallas kernels for 28%

profile of v1, /device:TPU:0, one launch (start us, length us, event | category | flops | bytes accessed | tf_op | source)
XLA Modules:
  0.0 280.3 jit_solution(5893190136460337376)
XLA Ops:
  0.6 0.9 dynamic-slice_bitcast_fusion
  1.6 3.1 %collective-permute-start = (bf16[1,96,768]{2,1,0:T(8,128)(2,1)S(1)}, bf16[1,96,768]{2,1,0:T(8,128)(2,1)S(1)}, u32[]{:S(2)}, u32[]{:S(2)}) collective-permute-start(bf16[1,96,768]{2,1,0:T(8,128)(2,1)S(1)} %dynamic-slice_bitcast_fusion), channel_id=1, source_target_pairs={{0,2},{1,3},{2,0},{3,1},{4,6},{5,7},{6,4},{7,5},{8,10},{9,11},{10,... | collective-permute-start | bytes 442376 | tf_op jit(solution)/shard_map/ppermute | solution.py:474
  4.7 1.3 fusion.16
  6.3 2.5 collective-permute-done
  8.8 3.0 %collective-permute-start.1 = (bf16[1,96,768]{2,1,0:T(8,128)(2,1)S(1)}, bf16[1,96,768]{2,1,0:T(8,128)(2,1)S(1)}, u32[]{:S(2)}, u32[]{:S(2)}) collective-permute-start(bf16[1,96,768]{2,1,0:T(8,128)(2,1)S(1)} %collective-permute-done), channel_id=1, source_target_pairs={{0,16},{4,20},{8,24},{12,28},{16,0},{20,4},{24,8},{28,12},{1,17},{... | collective-permute-start | bytes 442376 | tf_op jit(solution)/shard_map/ppermute | solution.py:474
  11.9 1.8 collective-permute-start.7
  13.9 1.8 collective-permute-start.8
  16.7 1.3 fusion.17
  19.9 1.7 collective-permute-done.3
  21.6 1.6 collective-permute-start.6
  23.8 15.0 %shard_map.254 = (bf16[1024,768]{1,0:T(8,128)(2,1)}, bf16[768,1024]{1,0:T(8,128)(2,1)}, bf16[1024,192]{1,0:T(8,128)(2,1)}, bf16[1024,192]{1,0:T(8,128)(2,1)}, bf...) custom-call(s32[7]{0:T(128)} %stack.100.refs_0_.info_ref, ...), custom_call_target="tpu_custom_call" | custom-call | flops 11000000512 | bytes 33000000 | tf_op jit(solution)/shard_map/pallas_call | solution.py:559
  40.3 15.4 %shard_map.255 = (bf16[1024,192]{1,0:T(8,128)(2,1)}, bf16[1024,192]{1,0:T(8,128)(2,1)}, bf16[1024,192]{1,0:T(8,128)(2,1)}, bf16[192,1024]{1,0:T(8,128)(2,1)}, bf...) custom-call(s32[7]{0:T(128)} %stack.100.refs_0_.info_ref, ...), custom_call_target="tpu_custom_call" | custom-call | flops 12000000000 | bytes 36000000 | tf_op jit(solution)/shard_map/pallas_call | solution.py:582
  56.1 1.6 collective-permute-start.12
  58.9 19.0 %collective-permute-done.11 = bf16[4,48,768]{2,1,0:T(8,128)(2,1)S(1)} collective-permute-done((bf16[4,48,768]{2,1,0:T(8,128)(2,1)S(1)}, bf16[4,48,768]{2,1,0:T(8,128)(2,1)S(1)}, u32[]{:S(2)}, u32[]{:S(2)}) %collective-permute-start.11) | collective-permute-done | bytes 294944 | tf_op jit(solution)/shard_map/ppermute | solution.py:474
  77.9 0.9 maximum_select_fusion.1
  78.8 1.1 maximum_select_fusion
  80.0 0.8 copy-done.15
  80.8 27.7 %shard_map.256 = (f32[1024,768]{1,0:T(8,128)}, bf16[1024,768]{1,0:T(8,128)(2,1)}, bf16[1024,768]{1,0:T(8,128)(2,1)}, bf16[2,4,96,768]{3,2,1,0:T(8,128)(2,1)}, bf...) custom-call(s32[7]{0:T(128)} %stack.100.refs_0_.info_ref, ...), custom_call_target="tpu_custom_call" | custom-call | flops 28000000000 | bytes 84000000 | tf_op jit(solution)/shard_map/pallas_call | solution.py:603
  109.1 1.5 collective-permute-start.24
  110.6 1.6 collective-permute-start.25
  112.3 2.2 collective-permute-done.16.refs_2_
  114.6 25.1 %shard_map.258 = (f32[1024,768]{1,0:T(8,128)}, bf16[1024,768]{1,0:T(8,128)(2,1)}, bf16[768,1024]{1,0:T(8,128)(2,1)}, f32[1024,768]{1,0:T(8,128)}, bf16[4,96,768]...) custom-call(s32[7]{0:T(128)} %stack.100.refs_0_.info_ref, ...), custom_call_target="tpu_custom_call" | custom-call | flops 20999999488 | bytes 63000000 | tf_op jit(solution)/shard_map/pallas_call | solution.py:659
  139.7 19.6 %shard_map.259 = (bf16[1024,768]{1,0:T(8,128)(2,1)}, bf16[4,96,768]{2,1,0:T(8,128)(2,1)}, bf16[4,96,768]{2,1,0:T(8,128)(2,1)}, f32[1,576]{1,0:T(1,128)}) custom-call(s32[7]{0:T(128)} %stack.100.refs_0_.info_ref, bf16[1024,768]{1,0:T(8,128)(2,1)} %get-tuple-element.94.refs_1_, f32[1024,768]{1,0:T(8,128)} %get-tuple-element.95.refs_2_, ...), custom_call_target="tpu_custom_call" | custom-call | flops 16999999488 | bytes 51000000 | tf_op jit(solution)/shard_map/pallas_call | solution.py:675
  159.5 1.5 collective-permute-start.27
  161.0 1.1 fusion.1
  162.2 1.7 collective-permute-start.32
  163.9 3.4 %shard_map.257 = bf16[512,768]{1,0:T(8,128)(2,1)} custom-call(s32[7]{0:T(128)} %stack.100.refs_0_.info_ref, f32[1024,768]{1,0:T(8,128)} %get-tuple-element.84.residual_ref.refs_3_, bf16[1024,768]{1,0:T(8,128)(2,1)} %get-tuple-element.85.mlp_a_ref.refs_6_, bf16[1024,768]{1,0:T(8,128)(2,1)} %collective-permute-done.13.mlp_b_ref.refs_7_, f32[768]{0:T(1024)} %refs_8_.1), custom_call_target="tpu_custom_call" | custom-call | flops 3000000000 | bytes 9000000 | tf_op jit(solution)/shard_map/pallas_call | solution.py:626
  167.8 1.0 fusion
  168.8 1.6 collective-permute-start.26
  170.4 5.0 %collective-permute-done.27 = bf16[4,96,768]{2,1,0:T(8,128)(2,1)} collective-permute-done((bf16[4,96,768]{2,1,0:T(8,128)(2,1)}, bf16[4,96,768]{2,1,0:T(8,128)(2,1)}, u32[]{:S(2)}, u32[]{:S(2)}) %collective-permute-start.27) | collective-permute-done | bytes 589856 | tf_op jit(solution)/shard_map/ppermute | solution.py:474
  175.4 1.5 collective-permute-start.29
  176.9 1.2 add_convert_fusion.1
  178.7 1.7 collective-permute-start.28
  180.4 1.3 bitcast_add_fusion.1
  181.7 0.8 fusion.3
  182.4 13.1 %collective-permute-done.14.near_ref = bf16[512,768]{1,0:T(8,128)(2,1)} collective-permute-done((bf16[512,768]{1,0:T(8,128)(2,1)}, bf16[512,768]{1,0:T(8,128)(2,1)}, u32[]{:S(2)}, u32[]{:S(2)}) %collective-permute-start.14) | collective-permute-done | bytes 786464 | tf_op jit(solution)/shard_map/ppermute | solution.py:474
  195.5 1.6 collective-permute-start.33
  197.1 7.6 %shard_map.260 = (f32[2048,768]{1,0:T(8,128)}, bf16[512,768]{1,0:T(8,128)(2,1)}, f32[8,768]{1,0:T(8,128)}, f32[8,768]{1,0:T(8,128)}) custom-call(s32[7]{0:T(128)} %stack.100.refs_0_.info_ref, bf16[2048,768]{1,0:T(8,128)(2,1)} %x_ref.1, bf16[1024,768]{1,0:T(8,128)(2,1)} %get-tuple-element.102.grad_a_ref, ...), custom_call_target="tpu_custom_call" | custom-call | flops 7000000000 | bytes 21000000 | tf_op jit(solution)/shard_map/pallas_call | solution.py:689
  204.7 3.4 %collective-permute-done.26 = bf16[2,192,768]{2,1,0:T(8,128)(2,1)} collective-permute-done((bf16[2,192,768]{2,1,0:T(8,128)(2,1)}, bf16[2,192,768]{2,1,0:T(8,128)(2,1)}, u32[]{:S(2)}, u32[]{:S(2)}) %collective-permute-start.26) | collective-permute-done | bytes 589856 | tf_op jit(solution)/shard_map/ppermute | solution.py:474
  208.2 1.7 collective-permute-start.18
  209.9 0.8 copy-done.9
  210.8 10.0 %collective-permute-done.28 = bf16[4,96,768]{2,1,0:T(8,128)(2,1)} collective-permute-done((bf16[4,96,768]{2,1,0:T(8,128)(2,1)S(1)}, bf16[4,96,768]{2,1,0:T(8,128)(2,1)}, u32[]{:S(2)}, u32[]{:S(2)}) %collective-permute-start.28) | collective-permute-done | bytes 589856 | tf_op jit(solution)/shard_map/ppermute | solution.py:474
  220.8 1.4 bitcast_add_fusion
  223.6 1.7 collective-permute-start.20
  225.3 1.0 bitcast_add_fusion.3
  227.0 10.2 %collective-permute-done.20 = f32[8,768]{1,0:T(8,128)S(1)} collective-permute-done((f32[8,768]{1,0:T(8,128)S(1)}, f32[8,768]{1,0:T(8,128)S(1)}, u32[]{:S(2)}, u32[]{:S(2)}) %collective-permute-start.20) | collective-permute-done | bytes 24608 | tf_op jit(solution)/shard_map/ppermute | solution.py:474
  237.8 1.3 convert_add_fusion
  239.1 2.0 collective-permute-done.21
  241.1 1.6 collective-permute-start.22
  243.3 2.0 collective-permute-done.22
  245.2 1.2 collective-permute-start.23
  246.4 4.5 %shard_map.261 = bf16[2048,768]{1,0:T(8,128)(2,1)} custom-call(s32[7]{0:T(128)} %stack.100.refs_0_.info_ref, bf16[512,768]{1,0:T(8,128)(2,1)} %collective-permute-done.14.near_ref, bf16[512,768]{1,0:T(8,128)(2,1)} %collective-permute-done.15.far_ref, bf16[2048,768]{1,0:T(8,128)(2,1)} %get-tuple-element.112.whole_ref), custom_call_target="tpu_custom_call", output_to_operand_aliasing={{}: (3, {})} | custom-call | flops 3000000000 | bytes 9000000 | tf_op jit(solution)/shard_map/pallas_call | solution.py:716
  253.8 1.4 reshape.324
  255.8 1.3 fusion.10
  257.1 1.7 bitcast_add_fusion.6
  258.9 1.8 collective-permute-start.31
  260.7 1.0 bitcast_add_fusion.2
  261.8 1.2 collective-permute-start.36
  263.0 3.6 %collective-permute-done.31 = bf16[96,768]{1,0:T(8,128)(2,1)S(1)} collective-permute-done((bf16[96,768]{1,0:T(8,128)(2,1)S(1)}, bf16[96,768]{1,0:T(8,128)(2,1)S(1)}, u32[]{:S(2)}, u32[]{:S(2)}) %collective-permute-start.31) | collective-permute-done | bytes 147488 | tf_op jit(solution)/shard_map/ppermute | solution.py:474
  266.7 0.9 copy.41
  268.4 4.5 %collective-permute-done.36 = bf16[96,768]{1,0:T(8,128)(2,1)S(1)} collective-permute-done((bf16[96,768]{1,0:T(8,128)(2,1)S(1)}, bf16[96,768]{1,0:T(8,128)(2,1)S(1)}, u32[]{:S(2)}, u32[]{:S(2)}) %collective-permute-start.36) | collective-permute-done | bytes 147488 | tf_op jit(solution)/shard_map/ppermute | solution.py:474
  273.6 2.9 %shard_map.262.whole_ref = f32[2048,768]{1,0:T(8,128)} custom-call(s32[7]{0:T(128)} %stack.100.refs_0_.info_ref, bf16[512,768]{1,0:T(8,128)(2,1)} %collective-permute-done.18.come_ref, f32[2048,768]{1,0:T(8,128)} %get-tuple-element.113.whole_ref), custom_call_target="tpu_custom_call", output_to_operand_aliasing={{}: (2, {})} | custom-call | flops 2000000000 | bytes 6000000 | tf_op jit(solution)/shard_map/pallas_call | solution.py:737
  276.5 0.9 copy-done.6
  277.4 2.9 %shard_map.263 = f32[2048,768]{1,0:T(8,128)} custom-call(s32[7]{0:T(128)} %stack.100.refs_0_.info_ref, bf16[512,768]{1,0:T(8,128)(2,1)} %copy-done.6, f32[2048,768]{1,0:T(8,128)} %shard_map.262.whole_ref), custom_call_target="tpu_custom_call", output_to_operand_aliasing={{}: (2, {})} | custom-call | flops 2000000000 | bytes 6000000 | tf_op jit(solution)/shard_map/pallas_call | solution.py:737
  (114 shorter events, 16.1 us)
Async XLA Ops:
  1.6 4.6 %copy-start.13 = (f32[2,3,64]{2,0,1:T(2,128)S(1)}, f32[2,3,64]{2,0,1:T(2,128)}, u32[]{:S(2)}) copy-start(f32[2,3,64]{2,0,1:T(2,128)} %param.20) | copy-start | bytes 4612
  1.6 4.7 %copy-start.12 = (f32[6,128]{1,0:T(8,128)S(1)}, f32[6,128]{1,0:T(8,128)}, u32[]{:S(2)}) copy-start(f32[6,128]{1,0:T(8,128)} %param.26) | copy-start | bytes 9220
  1.6 12.1 %copy-start.14 = (bf16[768,3,3,64]{0,3,2,1:T(8,128)(2,1)S(1)}, bf16[768,3,3,64]{0,3,2,1:T(8,128)(2,1)}, u32[]{:S(2)}) copy-start(bf16[768,3,3,64]{0,3,2,1:T(8,128)(2,1)} %param.19) | copy-start | bytes 2654212
  1.6 12.3 %copy-start.16 = (bf16[3,64,768]{2,1,0:T(8,128)(2,1)S(1)}, bf16[3,64,768]{2,1,0:T(8,128)(2,1)}, u32[]{:S(2)}) copy-start(bf16[3,64,768]{2,1,0:T(8,128)(2,1)} %param.21) | copy-start | bytes 884740
  1.6 7.2 %collective-permute-start = (bf16[1,96,768]{2,1,0:T(8,128)(2,1)S(1)}, bf16[1,96,768]{2,1,0:T(8,128)(2,1)S(1)}, u32[]{:S(2)}, u32[]{:S(2)}) collective-permute-start(bf16[1,96,768]{2,1,0:T(8,128)(2,1)S(1)} %dynamic-slice_bitcast_fusion), channel_id=1, source_target_pairs={{0,2},{1,3},{2,0},{3,1},{4,6},{5,7},{6,4},{7,5},{8,10},{9,11},{10,... | collective-permute-start | bytes 442376 | tf_op jit(solution)/shard_map/ppermute | solution.py:474
  6.0 10.3 %collective-permute-start.2 = (bf16[1,48,768]{2,1,0:T(8,128)(2,1)S(1)}, bf16[1,48,768]{2,1,0:T(8,128)(2,1)S(1)}, u32[]{:S(2)}, u32[]{:S(2)}) collective-permute-start(bf16[1,48,768]{2,1,0:T(8,128)(2,1)S(1)} %dynamic-slice_bitcast_fusion.1), channel_id=1, source_target_pairs={{0,2},{1,3},{2,0},{3,1},{4,6},{5,7},{6,4},{7,5},{8,10},{9,11},{10,... | collective-permute-start | bytes 221192 | tf_op jit(solution)/shard_map/ppermute | solution.py:474
  8.8 12.8 %collective-permute-start.1 = (bf16[1,96,768]{2,1,0:T(8,128)(2,1)S(1)}, bf16[1,96,768]{2,1,0:T(8,128)(2,1)S(1)}, u32[]{:S(2)}, u32[]{:S(2)}) collective-permute-start(bf16[1,96,768]{2,1,0:T(8,128)(2,1)S(1)} %collective-permute-done), channel_id=1, source_target_pairs={{0,16},{4,20},{8,24},{12,28},{16,0},{20,4},{24,8},{28,12},{1,17},{... | collective-permute-start | bytes 442376 | tf_op jit(solution)/shard_map/ppermute | solution.py:474
  11.9 27.0 %collective-permute-start.7 = (f32[1,1152]{1,0:T(1,128)S(1)}, f32[1,1152]{1,0:T(1,128)S(1)}, u32[]{:S(2)}, u32[]{:S(2)}) collective-permute-start(f32[1,1152]{1,0:T(1,128)S(1)} %pad_maximum_fusion.1), channel_id=1, source_target_pairs={{0,2},{1,3},{2,0},{3,1},{4,6},{5,7},{6,4},{7,5},{8,10},{9,11},{10,... | collective-permute-start | bytes 13832 | tf_op jit(solution)/shard_map/ppermute | solution.py:474
  13.7 25.9 %collective-permute-start.4 = (bf16[576,768]{1,0:T(8,128)(2,1)S(1)}, bf16[576,768]{1,0:T(8,128)(2,1)}, u32[]{:S(2)}, u32[]{:S(2)}) collective-permute-start(bf16[576,768]{1,0:T(8,128)(2,1)S(1)} %bitcast.129), channel_id=1, source_target_pairs={{0,2},{1,3},{2,0},{3,1},{4,6},{5,7},{6,4},{7,5},{8,10},{9,11},{10,... | collective-permute-start | bytes 2654216 | tf_op jit(solution)/shard_map/ppermute | solution.py:474
  13.9 25.7 %collective-permute-start.8 = (bf16[192,768]{1,0:T(8,128)(2,1)S(1)}, bf16[192,768]{1,0:T(8,128)(2,1)S(1)}, u32[]{:S(2)}, u32[]{:S(2)}) collective-permute-start(bf16[192,768]{1,0:T(8,128)(2,1)S(1)} %bitcast.132), channel_id=1, source_target_pairs={{0,2},{1,3},{2,0},{3,1},{4,6},{5,7},{6,4},{7,5},{8,10},{9,11},{10,... | collective-permute-start | bytes 884744 | tf_op jit(solution)/shard_map/ppermute | solution.py:474
  16.4 5.3 %collective-permute-start.3 = (bf16[1,48,768]{2,1,0:T(8,128)(2,1)S(1)}, bf16[1,48,768]{2,1,0:T(8,128)(2,1)S(1)}, u32[]{:S(2)}, u32[]{:S(2)}) collective-permute-start(bf16[1,48,768]{2,1,0:T(8,128)(2,1)S(1)} %collective-permute-done.2), channel_id=1, source_target_pairs={{0,16},{4,20},{8,24},{12,28},{16,0},{20,4},{24,8},{28,12},{1,17},{... | collective-permute-start | bytes 221192 | tf_op jit(solution)/shard_map/ppermute | solution.py:474
  21.6 17.2 %collective-permute-start.6 = (bf16[2,48,768]{2,1,0:T(8,128)(2,1)S(1)}, bf16[2,48,768]{2,1,0:T(8,128)(2,1)S(1)}, u32[]{:S(2)}, u32[]{:S(2)}) collective-permute-start(bf16[2,48,768]{2,1,0:T(8,128)(2,1)S(1)} %maximum_select_fusion.6), channel_id=1, source_target_pairs={{0,8},{4,12},{8,0},{12,4},{16,24},{20,28},{24,16},{28,20},{1,9},{5... | collective-permute-start | bytes 442376 | tf_op jit(solution)/shard_map/ppermute | solution.py:474
  23.3 15.6 %collective-permute-start.5 = (bf16[2,96,768]{2,1,0:T(8,128)(2,1)S(1)}, bf16[2,96,768]{2,1,0:T(8,128)(2,1)S(1)}, u32[]{:S(2)}, u32[]{:S(2)}) collective-permute-start(bf16[2,96,768]{2,1,0:T(8,128)(2,1)S(1)} %maximum_select_fusion.3), channel_id=1, source_target_pairs={{0,8},{4,12},{8,0},{12,4},{16,24},{20,28},{24,16},{28,20},{1,9},{5... | collective-permute-start | bytes 884744 | tf_op jit(solution)/shard_map/ppermute | solution.py:474
  39.6 0.7 copy-start.17
  55.7 24.3 %collective-permute-start.9 = (bf16[1024,768]{1,0:T(8,128)(2,1)}, bf16[1024,768]{1,0:T(8,128)(2,1)}, u32[]{:S(2)}, u32[]{:S(2)}) collective-permute-start(bf16[1024,768]{1,0:T(8,128)(2,1)} %get-tuple-element.81.branch_a_ref), channel_id=1, source_target_pairs={{0,1},{1,0},{2,3},{3,2},{4,5},{5,4},{6,7},{7,6},{8,9},{9,8},{10,11... | collective-permute-start | bytes 4718600 | tf_op jit(solution)/shard_map/ppermute | solution.py:474
  55.7 24.2 %collective-permute-start.10 = (bf16[384,768]{1,0:T(8,128)(2,1)S(1)}, bf16[384,768]{1,0:T(8,128)(2,1)S(1)}, u32[]{:S(2)}, u32[]{:S(2)}) collective-permute-start(bf16[384,768]{1,0:T(8,128)(2,1)S(1)} %get-tuple-element.150), channel_id=1, source_target_pairs={{0,2},{1,3},{2,0},{3,1},{4,6},{5,7},{6,4},{7,5},{8,10},{9,11},{10,... | collective-permute-start | bytes 1769480 | tf_op jit(solution)/shard_map/ppermute | solution.py:474
  56.1 22.7 %collective-permute-start.12 = (bf16[4,96,768]{2,1,0:T(8,128)(2,1)S(1)}, bf16[4,96,768]{2,1,0:T(8,128)(2,1)S(1)}, u32[]{:S(2)}, u32[]{:S(2)}) collective-permute-start(bf16[4,96,768]{2,1,0:T(8,128)(2,1)S(1)} %bitcast.107), channel_id=1, source_target_pairs={{0,4},{4,0},{8,12},{12,8},{16,20},{20,16},{24,28},{28,24},{1,5},{5... | collective-permute-start | bytes 1769480 | tf_op jit(solution)/shard_map/ppermute | solution.py:474
  57.7 20.2 %collective-permute-start.11 = (bf16[4,48,768]{2,1,0:T(8,128)(2,1)S(1)}, bf16[4,48,768]{2,1,0:T(8,128)(2,1)S(1)}, u32[]{:S(2)}, u32[]{:S(2)}) collective-permute-start(bf16[4,48,768]{2,1,0:T(8,128)(2,1)S(1)} %bitcast.110), channel_id=1, source_target_pairs={{0,4},{4,0},{8,12},{12,8},{16,20},{20,16},{24,28},{28,24},{1,5},{5... | collective-permute-start | bytes 884744 | tf_op jit(solution)/shard_map/ppermute | solution.py:474
  80.0 0.8 copy-start.15
  108.5 3.8 %collective-permute-start.13 = (bf16[1024,768]{1,0:T(8,128)(2,1)}, bf16[1024,768]{1,0:T(8,128)(2,1)}, u32[]{:S(2)}, u32[]{:S(2)}) collective-permute-start(bf16[1024,768]{1,0:T(8,128)(2,1)} %get-tuple-element.85.mlp_a_ref.refs_6_), channel_id=1, source_target_pairs={{0,1},{1,0},{2,3},{3,2},{4,5},{5,4},{6,7},{7,6},{8,9},{9,8},{10,11... | collective-permute-start | bytes 4718600 | tf_op jit(solution)/shard_map/ppermute | solution.py:474
  108.6 6.0 %collective-permute-start.16 = (bf16[1024,768]{1,0:T(8,128)(2,1)}, bf16[1024,768]{1,0:T(8,128)(2,1)}, u32[]{:S(2)}, u32[]{:S(2)}) collective-permute-start(bf16[1024,768]{1,0:T(8,128)(2,1)} %get-tuple-element.86.refs_1_), channel_id=1, source_target_pairs={{0,1},{1,0},{2,3},{3,2},{4,5},{5,4},{6,7},{7,6},{8,9},{9,8},{10,11... | collective-permute-start | bytes 4718600 | tf_op jit(solution)/shard_map/ppermute | solution.py:474
  109.1 51.9 %collective-permute-start.24 = (bf16[2,4,96,768]{3,2,1,0:T(8,128)(2,1)}, bf16[2,4,96,768]{3,2,1,0:T(8,128)(2,1)S(1)}, u32[]{:S(2)}, u32[]{:S(2)}) collective-permute-start(bf16[2,4,96,768]{3,2,1,0:T(8,128)(2,1)} %get-tuple-element.118), channel_id=1, source_target_pairs={{0,4},{4,0},{8,12},{12,8},{16,20},{20,16},{24,28},{28,24},{1,5},{5... | collective-permute-start | bytes 3538952 | tf_op jit(solution)/shard_map/ppermute | solution.py:474
  110.6 50.5 %collective-permute-start.25 = (bf16[2,2,192,768]{3,2,1,0:T(8,128)(2,1)}, bf16[2,2,192,768]{3,2,1,0:T(8,128)(2,1)S(1)}, u32[]{:S(2)}, u32[]{:S(2)}) collective-permute-start(bf16[2,2,192,768]{3,2,1,0:T(8,128)(2,1)} %get-tuple-element.119), channel_id=1, source_target_pairs={{0,8},{4,12},{8,0},{12,4},{16,24},{20,28},{24,16},{28,20},{1,9},{5... | collective-permute-start | bytes 3538952 | tf_op jit(solution)/shard_map/ppermute | solution.py:474
  139.7 21.4 %copy-start.2 = (bf16[2,4,96,768]{3,2,1,0:T(8,128)(2,1)S(1)}, bf16[2,4,96,768]{3,2,1,0:T(8,128)(2,1)}, u32[]{:S(2)}) copy-start(bf16[2,4,96,768]{3,2,1,0:T(8,128)(2,1)} %get-tuple-element.128) | copy-start | bytes 3538948
  159.3 37.8 %collective-permute-start.17 = (bf16[1024,768]{1,0:T(8,128)(2,1)}, bf16[1024,768]{1,0:T(8,128)(2,1)}, u32[]{:S(2)}, u32[]{:S(2)}) collective-permute-start(bf16[1024,768]{1,0:T(8,128)(2,1)} %get-tuple-element.102.grad_a_ref), channel_id=1, source_target_pairs={{0,1},{1,0},{2,3},{3,2},{4,5},{5,4},{6,7},{7,6},{8,9},{9,8},{10,11... | collective-permute-start | bytes 4718600 | tf_op jit(solution)/shard_map/ppermute | solution.py:474
  159.5 15.9 %collective-permute-start.27 = (bf16[4,96,768]{2,1,0:T(8,128)(2,1)}, bf16[4,96,768]{2,1,0:T(8,128)(2,1)}, u32[]{:S(2)}, u32[]{:S(2)}) collective-permute-start(bf16[4,96,768]{2,1,0:T(8,128)(2,1)} %get-tuple-element.122), channel_id=1, source_target_pairs={{0,4},{4,0},{8,12},{12,8},{16,20},{20,16},{24,28},{28,24},{1,5},{5... | collective-permute-start | bytes 1769480 | tf_op jit(solution)/shard_map/ppermute | solution.py:474
  161.0 6.3 %copy-start.4 = (bf16[2,4,96,768]{3,2,1,0:T(8,128)(2,1)}, bf16[2,4,96,768]{3,2,1,0:T(8,128)(2,1)S(1)}, u32[]{:S(2)}) copy-start(bf16[2,4,96,768]{3,2,1,0:T(8,128)(2,1)S(1)} %collective-permute-done.24) | copy-start | bytes 3538948
  161.0 6.8 %copy-start.1 = (bf16[2,2,192,768]{3,2,1,0:T(8,128)(2,1)}, bf16[2,2,192,768]{3,2,1,0:T(8,128)(2,1)S(1)}, u32[]{:S(2)}) copy-start(bf16[2,2,192,768]{3,2,1,0:T(8,128)(2,1)S(1)} %collective-permute-done.25) | copy-start | bytes 3538948
  162.2 5.7 %copy-start = (bf16[2,2,192,768]{3,2,1,0:T(8,128)(2,1)S(1)}, bf16[2,2,192,768]{3,2,1,0:T(8,128)(2,1)}, u32[]{:S(2)}) copy-start(bf16[2,2,192,768]{3,2,1,0:T(8,128)(2,1)} %get-tuple-element.117) | copy-start | bytes 3538948
  162.2 16.5 %collective-permute-start.32 = (bf16[4,96,768]{2,1,0:T(8,128)(2,1)}, bf16[4,96,768]{2,1,0:T(8,128)(2,1)}, u32[]{:S(2)}, u32[]{:S(2)}) collective-permute-start(bf16[4,96,768]{2,1,0:T(8,128)(2,1)} %fusion.1), channel_id=1, source_target_pairs={{0,2},{1,3},{2,0},{3,1},{4,6},{5,7},{6,4},{7,5},{8,10},{9,11},{10,... | collective-permute-start | bytes 1769480 | tf_op jit(solution)/shard_map/ppermute | solution.py:474
  167.3 9.6 %copy-start.7 = (bf16[4,96,768]{2,1,0:T(8,128)(2,1)S(1)}, bf16[4,96,768]{2,1,0:T(8,128)(2,1)}, u32[]{:S(2)}) copy-start(bf16[4,96,768]{2,1,0:T(8,128)(2,1)} %get-tuple-element.121) | copy-start | bytes 1769476
  167.3 28.2 %collective-permute-start.14 = (bf16[512,768]{1,0:T(8,128)(2,1)}, bf16[512,768]{1,0:T(8,128)(2,1)}, u32[]{:S(2)}, u32[]{:S(2)}) collective-permute-start(bf16[512,768]{1,0:T(8,128)(2,1)} %shard_map.257), channel_id=1, source_target_pairs={{0,2},{1,3},{2,0},{3,1},{4,6},{5,7},{6,4},{7,5},{8,10},{9,11},{10,... | collective-permute-start | bytes 2359304 | tf_op jit(solution)/shard_map/ppermute | solution.py:474
  167.8 12.6 %copy-start.5 = (bf16[2,4,96,768]{3,2,1,0:T(8,128)(2,1)S(1)}, bf16[2,4,96,768]{3,2,1,0:T(8,128)(2,1)}, u32[]{:S(2)}) copy-start(bf16[2,4,96,768]{3,2,1,0:T(8,128)(2,1)} %copy-done.4) | copy-start | bytes 3538948
  168.8 11.6 %copy-start.3 = (bf16[2,4,96,768]{3,2,1,0:T(8,128)(2,1)S(1)}, bf16[2,4,96,768]{3,2,1,0:T(8,128)(2,1)}, u32[]{:S(2)}) copy-start(bf16[2,4,96,768]{3,2,1,0:T(8,128)(2,1)} %get-tuple-element.128) | copy-start | bytes 3538948
  168.8 39.3 %collective-permute-start.26 = (bf16[2,192,768]{2,1,0:T(8,128)(2,1)}, bf16[2,192,768]{2,1,0:T(8,128)(2,1)}, u32[]{:S(2)}, u32[]{:S(2)}) collective-permute-start(bf16[2,192,768]{2,1,0:T(8,128)(2,1)} %fusion), channel_id=1, source_target_pairs={{0,2},{1,3},{2,0},{3,1},{4,6},{5,7},{6,4},{7,5},{8,10},{9,11},{10,... | collective-permute-start | bytes 1769480 | tf_op jit(solution)/shard_map/ppermute | solution.py:474
  175.4 34.5 %collective-permute-start.29 = (bf16[4,96,768]{2,1,0:T(8,128)(2,1)}, bf16[4,96,768]{2,1,0:T(8,128)(2,1)S(1)}, u32[]{:S(2)}, u32[]{:S(2)}) collective-permute-start(bf16[4,96,768]{2,1,0:T(8,128)(2,1)} %get-tuple-element.124), channel_id=1, source_target_pairs={{0,4},{4,0},{8,12},{12,8},{16,20},{20,16},{24,28},{28,24},{1,5},{5... | collective-permute-start | bytes 1769480 | tf_op jit(solution)/shard_map/ppermute | solution.py:474
  178.7 42.1 %collective-permute-start.28 = (bf16[4,96,768]{2,1,0:T(8,128)(2,1)S(1)}, bf16[4,96,768]{2,1,0:T(8,128)(2,1)}, u32[]{:S(2)}, u32[]{:S(2)}) collective-permute-start(bf16[4,96,768]{2,1,0:T(8,128)(2,1)S(1)} %add_convert_fusion.1), channel_id=1, source_target_pairs={{0,2},{1,3},{2,0},{3,1},{4,6},{5,7},{6,4},{7,5},{8,10},{9,11},{10,... | collective-permute-start | bytes 1769480 | tf_op jit(solution)/shard_map/ppermute | solution.py:474
  195.5 28.0 %collective-permute-start.33 = (bf16[2,96,768]{2,1,0:T(8,128)(2,1)}, bf16[2,96,768]{2,1,0:T(8,128)(2,1)}, u32[]{:S(2)}, u32[]{:S(2)}) collective-permute-start(bf16[2,96,768]{2,1,0:T(8,128)(2,1)} %fusion.3), channel_id=1, source_target_pairs={{0,8},{4,12},{8,0},{12,4},{16,24},{20,28},{24,16},{28,20},{1,9},{5... | collective-permute-start | bytes 884744 | tf_op jit(solution)/shard_map/ppermute | solution.py:474
  197.1 45.6 %collective-permute-start.15 = (bf16[512,768]{1,0:T(8,128)(2,1)}, bf16[512,768]{1,0:T(8,128)(2,1)}, u32[]{:S(2)}, u32[]{:S(2)}) collective-permute-start(bf16[512,768]{1,0:T(8,128)(2,1)} %collective-permute-done.14.near_ref), channel_id=1, source_target_pairs={{0,1},{1,0},{2,3},{3,2},{4,5},{5,4},{6,7},{7,6},{8,9},{9,8},{10,11... | collective-permute-start | bytes 2359304 | tf_op jit(solution)/shard_map/ppermute | solution.py:474
  208.2 15.4 %copy-start.18 = (f32[8,768]{1,0:T(8,128)S(1)}, f32[8,768]{1,0:T(8,128)}, u32[]{:S(2)}) copy-start(f32[8,768]{1,0:T(8,128)} %get-tuple-element.115) | copy-start | bytes 73732
  208.2 52.5 %collective-permute-start.18 = (bf16[512,768]{1,0:T(8,128)(2,1)}, bf16[512,768]{1,0:T(8,128)(2,1)}, u32[]{:S(2)}, u32[]{:S(2)}) collective-permute-start(bf16[512,768]{1,0:T(8,128)(2,1)} %get-tuple-element.109), channel_id=1, source_target_pairs={{0,2},{1,3},{2,0},{3,1},{4,6},{5,7},{6,4},{7,5},{8,10},{9,11},{10,... | collective-permute-start | bytes 2359304 | tf_op jit(solution)/shard_map/ppermute | solution.py:474
  209.9 0.8 copy-start.9
  222.3 15.0 %copy-start.11 = (f32[8,768]{1,0:T(8,128)S(1)}, f32[8,768]{1,0:T(8,128)}, u32[]{:S(2)}) copy-start(f32[8,768]{1,0:T(8,128)} %get-tuple-element.114) | copy-start | bytes 73732
  222.3 15.6 %copy-start.8 = (bf16[4,96,768]{2,1,0:T(8,128)(2,1)S(1)}, bf16[4,96,768]{2,1,0:T(8,128)(2,1)}, u32[]{:S(2)}) copy-start(bf16[4,96,768]{2,1,0:T(8,128)(2,1)} %get-tuple-element.116) | copy-start | bytes 1769476
  222.3 15.6 %copy-start.10 = (bf16[4,96,768]{2,1,0:T(8,128)(2,1)S(1)}, bf16[4,96,768]{2,1,0:T(8,128)(2,1)}, u32[]{:S(2)}) copy-start(bf16[4,96,768]{2,1,0:T(8,128)(2,1)} %copy-done.9) | copy-start | bytes 1769476
  223.0 35.8 %collective-permute-start.35 = (bf16[2,96,768]{2,1,0:T(8,128)(2,1)}, bf16[2,96,768]{2,1,0:T(8,128)(2,1)}, u32[]{:S(2)}, u32[]{:S(2)}) collective-permute-start(bf16[2,96,768]{2,1,0:T(8,128)(2,1)} %fusion.4), channel_id=1, source_target_pairs={{0,4},{4,0},{8,12},{12,8},{16,20},{20,16},{24,28},{28,24},{1,5},{5... | collective-permute-start | bytes 884744 | tf_op jit(solution)/shard_map/ppermute | solution.py:474
  223.6 13.6 %collective-permute-start.20 = (f32[8,768]{1,0:T(8,128)S(1)}, f32[8,768]{1,0:T(8,128)S(1)}, u32[]{:S(2)}, u32[]{:S(2)}) collective-permute-start(f32[8,768]{1,0:T(8,128)S(1)} %copy-done.18), channel_id=1, source_target_pairs={{0,2},{1,3},{2,0},{3,1},{4,6},{5,7},{6,4},{7,5},{8,10},{9,11},{10,... | collective-permute-start | bytes 73736 | tf_op jit(solution)/shard_map/ppermute | solution.py:474
  227.0 30.1 %collective-permute-start.34 = (bf16[96,768]{1,0:T(8,128)(2,1)}, bf16[96,768]{1,0:T(8,128)(2,1)}, u32[]{:S(2)}, u32[]{:S(2)}) collective-permute-start(bf16[96,768]{1,0:T(8,128)(2,1)} %fusion.8), channel_id=1, source_target_pairs={{0,16},{4,20},{8,24},{12,28},{16,0},{20,4},{24,8},{28,12},{1,17},{... | collective-permute-start | bytes 442376 | tf_op jit(solution)/shard_map/ppermute | solution.py:474
  237.2 3.9 %collective-permute-start.21 = (f32[8,768]{1,0:T(8,128)S(1)}, f32[8,768]{1,0:T(8,128)S(1)}, u32[]{:S(2)}, u32[]{:S(2)}) collective-permute-start(f32[8,768]{1,0:T(8,128)S(1)} %add.118), channel_id=1, source_target_pairs={{0,4},{4,0},{8,12},{12,8},{16,20},{20,16},{24,28},{28,24},{1,5},{5... | collective-permute-start | bytes 73736 | tf_op jit(solution)/shard_map/ppermute | solution.py:474
  241.1 4.1 %collective-permute-start.22 = (f32[8,768]{1,0:T(8,128)S(1)}, f32[8,768]{1,0:T(8,128)S(1)}, u32[]{:S(2)}, u32[]{:S(2)}) collective-permute-start(f32[8,768]{1,0:T(8,128)S(1)} %add.119), channel_id=1, source_target_pairs={{0,8},{4,12},{8,0},{12,4},{16,24},{20,28},{24,16},{28,20},{1,9},{5... | collective-permute-start | bytes 73736 | tf_op jit(solution)/shard_map/ppermute | solution.py:474
  242.8 16.1 %collective-permute-start.30 = (bf16[2,96,768]{2,1,0:T(8,128)(2,1)S(1)}, bf16[2,96,768]{2,1,0:T(8,128)(2,1)S(1)}, u32[]{:S(2)}, u32[]{:S(2)}) collective-permute-start(bf16[2,96,768]{2,1,0:T(8,128)(2,1)S(1)} %fusion.2), channel_id=1, source_target_pairs={{0,8},{4,12},{8,0},{12,4},{16,24},{20,28},{24,16},{28,20},{1,9},{5... | collective-permute-start | bytes 884744 | tf_op jit(solution)/shard_map/ppermute | solution.py:474
  245.2 5.7 %collective-permute-start.23 = (f32[8,768]{1,0:T(8,128)S(1)}, f32[8,768]{1,0:T(8,128)S(1)}, u32[]{:S(2)}, u32[]{:S(2)}) collective-permute-start(f32[8,768]{1,0:T(8,128)S(1)} %add.120), channel_id=1, source_target_pairs={{0,16},{4,20},{8,24},{12,28},{16,0},{20,4},{24,8},{28,12},{1,17},{... | collective-permute-start | bytes 73736 | tf_op jit(solution)/shard_map/ppermute | solution.py:474
  258.9 7.7 %collective-permute-start.31 = (bf16[96,768]{1,0:T(8,128)(2,1)S(1)}, bf16[96,768]{1,0:T(8,128)(2,1)S(1)}, u32[]{:S(2)}, u32[]{:S(2)}) collective-permute-start(bf16[96,768]{1,0:T(8,128)(2,1)S(1)} %fusion.7), channel_id=1, source_target_pairs={{0,16},{4,20},{8,24},{12,28},{16,0},{20,4},{24,8},{28,12},{1,17},{... | collective-permute-start | bytes 442376 | tf_op jit(solution)/shard_map/ppermute | solution.py:474
  260.7 15.8 %collective-permute-start.19 = (bf16[512,768]{1,0:T(8,128)(2,1)}, bf16[512,768]{1,0:T(8,128)(2,1)S(1)}, u32[]{:S(2)}, u32[]{:S(2)}) collective-permute-start(bf16[512,768]{1,0:T(8,128)(2,1)} %collective-permute-done.18.come_ref), channel_id=1, source_target_pairs={{0,1},{1,0},{2,3},{3,2},{4,5},{5,4},{6,7},{7,6},{8,9},{9,8},{10,11... | collective-permute-start | bytes 2359304 | tf_op jit(solution)/shard_map/ppermute | solution.py:474
  261.8 11.1 %collective-permute-start.36 = (bf16[96,768]{1,0:T(8,128)(2,1)S(1)}, bf16[96,768]{1,0:T(8,128)(2,1)S(1)}, u32[]{:S(2)}, u32[]{:S(2)}) collective-permute-start(bf16[96,768]{1,0:T(8,128)(2,1)S(1)} %fusion.9), channel_id=1, source_target_pairs={{0,16},{4,20},{8,24},{12,28},{16,0},{20,4},{24,8},{28,12},{1,17},{... | collective-permute-start | bytes 442376 | tf_op jit(solution)/shard_map/ppermute | solution.py:474
  276.5 0.9 copy-start.6

commit v2 on v1

--- a/solution.py
+++ b/solution.py
@@ -104,9 +104,36 @@
     return attended, [row_max + jnp.log(total) for row_max, total, _ in state]
 
 
+def attend_rows(queries, keys_ref, values_t_ref, start, old_rows, heads, head_dim):
+    width = heads * head_dim
+    allowed = allowed_diagonal()
+    here = pl.ds(start, QUERY_ROWS)
+    attended_t = []
+    logs = []
+    for head in range(heads):
+        query = head_lanes(queries, head, head_dim)
+        lanes = group_lanes(head, head_dim, width)
+        rows = slice(head * head_dim, (head + 1) * head_dim)
+        near = jnp.where(allowed, dot_nt(keys_ref[here, lanes], query), MASKED)
+        row_max = jnp.max(near, axis=0, keepdims=True)
+        if old_rows:
+            far = dot_nt(keys_ref[0:old_rows, lanes], query)
+            row_max = jnp.maximum(row_max, jnp.max(far, axis=0, keepdims=True))
+        near = jnp.exp(near - row_max)
+        total = jnp.sum(near, axis=0, keepdims=True)
+        summed = dot_nn(values_t_ref[rows, here], near.astype(BF16))
+        if old_rows:
+            far = jnp.exp(far - row_max)
+            total = total + jnp.sum(far, axis=0, keepdims=True)
+            summed = summed + dot_nn(values_t_ref[rows, 0:old_rows], far.astype(BF16))
+        attended_t.append(summed / total)
+        logs.append(row_max + jnp.log(total))
+    return jnp.concatenate(attended_t, axis=0).T, logs
+
+
 def attend_body(
     heads, head_dim, block, first_in, w_ref, bias_ref, mix_refs, att_ref, log_ref, keys_ref,
-    values_t_ref, is_long,
+    values_t_ref, is_long, unrolled,
 ):
     width = heads * head_dim
     projected = dot_nt(first_in, w_ref[...])
@@ -123,11 +150,26 @@
     values_t_ref[:, pl.ds(start, QUERY_ROWS)] = value_rows.T
     scaled = queries * jnp.asarray(1.0 / math.sqrt(head_dim), BF16)
 
-    attended, logs = attend_block(
-        scaled, keys_ref, values_t_ref, start, block * is_long, heads, head_dim
-    )
-    att_ref[...] = attended.astype(BF16)
-    log_ref[...] = jnp.concatenate(logs + [jnp.zeros((8 - heads, QUERY_ROWS), F32)], axis=0)
+
+    def finish(attended, logs):
+        att_ref[...] = attended.astype(BF16)
+        log_ref[...] = jnp.concatenate(logs + [jnp.zeros((8 - heads, QUERY_ROWS), F32)], axis=0)
+
+    if not unrolled:
+        finish(*attend_block(
+            scaled, keys_ref, values_t_ref, start, block * is_long, heads, head_dim
+        ))
+        return
+
+    @pl.when(block * is_long == 0)
+    def _():
+        finish(*attend_rows(scaled, keys_ref, values_t_ref, start, 0, heads, head_dim))
+
+    for position in range(1, keys_ref.shape[0] // QUERY_ROWS):
+
+        @pl.when(block * is_long == position)
+        def _(first=position * QUERY_ROWS):
+            finish(*attend_rows(scaled, keys_ref, values_t_ref, first, first, heads, head_dim))
 
 
 def forward_own_kernel(heads, head_dim, info_ref, x_ref, gain_ref, shift_ref, w_ref, bias_ref,
@@ -139,7 +181,7 @@
     first_t_ref[...] = first_in.T
     attend_body(heads, head_dim, pl.program_id(0), first_in, w_ref, bias_ref,
                 (query_ref, key_ref, value_ref, keys_t_ref), att_ref, log_ref, keys_ref,
-                values_t_ref, info_ref[1])
+                values_t_ref, info_ref[1], True)
 
 
 def forward_other_kernel(heads, head_dim, info_ref, first_ref, w_ref, bias_ref, att_own_ref,
@@ -147,7 +189,7 @@
                          att_ref, log_ref, branch_ref, keys_ref, values_t_ref):
     attend_body(heads, head_dim, pl.program_id(0), first_ref[...], w_ref, bias_ref,
                 (query_ref, key_ref, value_ref, keys_t_ref), att_ref, log_ref, keys_ref,
-                values_t_ref, info_ref[1])
+                values_t_ref, info_ref[1], True)
     branch = dot_nn(att_own_ref[...], w_out_own_ref[...]) + dot_nn(att_ref[...], w_out_ref[...])
     branch_ref[...] = branch.astype(BF16)
 

time: 281 us -> 278 us (0.989)
  Pallas kernels: 124 us -> 119 us
  waiting for transfers between devices: 80.1 us -> 83.7 us
    ppermute x37, waiting for transfers between devices: 80.1 us -> 83.7 us  [exchange(): return lax.ppermute(value, axis_name, [(i, i ^ bit) for i in range(size)])]
  transfers between devices with their start and end apart: 37 -> 37, of which waited for: 15 -> 17; matrix products, arithmetic and copies ran while one was open for 11% -> 11% of each run, Pallas kernels for 28% -> 27%
where the time goes in v2:
time: 278 us; the launch traced here: 277 us
  Pallas kernels  119 us (43%)
  waiting for transfers between devices  83.7 us (30%)
  starting transfers between devices  38.2 us (14%)
  local copies, waits for them, and re-layouts  18.5 us (7%)
  other arithmetic  15.2 us (5%)
    ppermute x37, waiting for transfers between devices, exchange(): return lax.ppermute(value, axis_name, [(i, i ^ bit) for i in range(size)])  83.7 us
    ppermute x37, starting transfers between devices, exchange(): return lax.ppermute(value, axis_name, [(i, i ^ bit) for i in range(size)])  38.2 us
    pallas_call x1, Pallas kernels, body(): call(mlp_kernel, blocks, [row_spec(QUERY_ROWS, width, True), first_spec,...  27.7 us
    pallas_call x1, Pallas kernels, body(): call(backward_other, blocks, [back_rows, back_rows, back_rows, back_spec(...  25.1 us
    pallas_call x1, Pallas kernels, body(): call(backward_own, blocks, [back_rows, back_rows] + back_mix + [in_place,...  19.6 us
    pallas_call x1, Pallas kernels, body(): call(forward_other, blocks, [first_spec, whole((3 * local, width)), whole...  12.7 us
    pallas_call x1, Pallas kernels, body(): call(forward_own, blocks, [row_spec(QUERY_ROWS, width, True), whole((widt...  12.3 us
    add x7, other arithmetic, add(): return kept.astype(F32) + received.astype(F32)  7.68 us
  transfers between devices with their start and end apart: 37, of which 17 were waited for; matrix products, arithmetic and copies ran while one was open for 11% of the time, Pallas kernels for 27%

profile of v2, /device:TPU:0, one launch (start us, length us, event | category | flops | bytes accessed | tf_op | source)
XLA Modules:
  0.0 276.6 jit_solution(2053408342910973804)
XLA Ops:
  0.6 0.9 dynamic-slice_bitcast_fusion
  1.6 3.1 %collective-permute-start = (bf16[1,96,768]{2,1,0:T(8,128)(2,1)S(1)}, bf16[1,96,768]{2,1,0:T(8,128)(2,1)S(1)}, u32[]{:S(2)}, u32[]{:S(2)}) collective-permute-start(bf16[1,96,768]{2,1,0:T(8,128)(2,1)S(1)} %dynamic-slice_bitcast_fusion), channel_id=1, source_target_pairs={{0,2},{1,3},{2,0},{3,1},{4,6},{5,7},{6,4},{7,5},{8,10},{9,11},{10,... | collective-permute-start | bytes 442376 | tf_op jit(solution)/shard_map/ppermute | solution.py:516
  4.7 1.3 fusion.16
  6.3 2.5 collective-permute-done
  8.8 3.0 %collective-permute-start.1 = (bf16[1,96,768]{2,1,0:T(8,128)(2,1)S(1)}, bf16[1,96,768]{2,1,0:T(8,128)(2,1)S(1)}, u32[]{:S(2)}, u32[]{:S(2)}) collective-permute-start(bf16[1,96,768]{2,1,0:T(8,128)(2,1)S(1)} %collective-permute-done), channel_id=1, source_target_pairs={{0,16},{4,20},{8,24},{12,28},{16,0},{20,4},{24,8},{28,12},{1,17},{... | collective-permute-start | bytes 442376 | tf_op jit(solution)/shard_map/ppermute | solution.py:516
  11.9 1.8 collective-permute-start.7
  13.9 1.8 collective-permute-start.8
  16.7 1.3 fusion.17
  19.9 1.7 collective-permute-done.3
  21.6 1.6 collective-permute-start.6
  23.8 12.3 %shard_map.254 = (bf16[1024,768]{1,0:T(8,128)(2,1)}, bf16[768,1024]{1,0:T(8,128)(2,1)}, bf16[1024,192]{1,0:T(8,128)(2,1)}, bf16[1024,192]{1,0:T(8,128)(2,1)}, bf...) custom-call(s32[7]{0:T(128)} %stack.100.refs_0_.info_ref, ...), custom_call_target="tpu_custom_call" | custom-call | flops 11000000512 | bytes 33000000 | tf_op jit(solution)/shard_map/pallas_call | solution.py:601
  36.8 2.4 collective-permute-done.8.refs_6_.refs_16_
  39.9 12.7 %shard_map.255 = (bf16[1024,192]{1,0:T(8,128)(2,1)}, bf16[1024,192]{1,0:T(8,128)(2,1)}, bf16[1024,192]{1,0:T(8,128)(2,1)}, bf16[192,1024]{1,0:T(8,128)(2,1)}, bf...) custom-call(s32[7]{0:T(128)} %stack.100.refs_0_.info_ref, ...), custom_call_target="tpu_custom_call" | custom-call | flops 12000000000 | bytes 36000000 | tf_op jit(solution)/shard_map/pallas_call | solution.py:624
  53.3 1.6 collective-permute-start.12
  56.1 18.9 %collective-permute-done.11 = bf16[4,48,768]{2,1,0:T(8,128)(2,1)S(1)} collective-permute-done((bf16[4,48,768]{2,1,0:T(8,128)(2,1)S(1)}, bf16[4,48,768]{2,1,0:T(8,128)(2,1)S(1)}, u32[]{:S(2)}, u32[]{:S(2)}) %collective-permute-start.11) | collective-permute-done | bytes 294944 | tf_op jit(solution)/shard_map/ppermute | solution.py:516
  75.1 0.9 maximum_select_fusion.1
  76.0 1.1 maximum_select_fusion
  77.1 0.8 copy-done.15
  77.9 27.7 %shard_map.256 = (f32[1024,768]{1,0:T(8,128)}, bf16[1024,768]{1,0:T(8,128)(2,1)}, bf16[1024,768]{1,0:T(8,128)(2,1)}, bf16[2,4,96,768]{3,2,1,0:T(8,128)(2,1)}, bf...) custom-call(s32[7]{0:T(128)} %stack.100.refs_0_.info_ref, ...), custom_call_target="tpu_custom_call" | custom-call | flops 28000000000 | bytes 84000000 | tf_op jit(solution)/shard_map/pallas_call | solution.py:645
  106.2 1.5 collective-permute-start.24
  107.7 1.6 collective-permute-start.25
  109.4 2.2 collective-permute-done.16.refs_2_
  111.7 25.1 %shard_map.258 = (f32[1024,768]{1,0:T(8,128)}, bf16[1024,768]{1,0:T(8,128)(2,1)}, bf16[768,1024]{1,0:T(8,128)(2,1)}, f32[1024,768]{1,0:T(8,128)}, bf16[4,96,768]...) custom-call(s32[7]{0:T(128)} %stack.100.refs_0_.info_ref, ...), custom_call_target="tpu_custom_call" | custom-call | flops 20999999488 | bytes 63000000 | tf_op jit(solution)/shard_map/pallas_call | solution.py:701
  136.8 19.6 %shard_map.259 = (bf16[1024,768]{1,0:T(8,128)(2,1)}, bf16[4,96,768]{2,1,0:T(8,128)(2,1)}, bf16[4,96,768]{2,1,0:T(8,128)(2,1)}, f32[1,576]{1,0:T(1,128)}) custom-call(s32[7]{0:T(128)} %stack.100.refs_0_.info_ref, bf16[1024,768]{1,0:T(8,128)(2,1)} %get-tuple-element.94.refs_1_, f32[1024,768]{1,0:T(8,128)} %get-tuple-element.95.refs_2_, ...), custom_call_target="tpu_custom_call" | custom-call | flops 16999999488 | bytes 51000000 | tf_op jit(solution)/shard_map/pallas_call | solution.py:717
  156.6 1.5 collective-permute-start.27
  158.2 1.1 fusion.1
  159.3 1.5 collective-permute-start.32
  160.8 3.4 %shard_map.257 = bf16[512,768]{1,0:T(8,128)(2,1)} custom-call(s32[7]{0:T(128)} %stack.100.refs_0_.info_ref, f32[1024,768]{1,0:T(8,128)} %get-tuple-element.84.residual_ref.refs_3_, bf16[1024,768]{1,0:T(8,128)(2,1)} %get-tuple-element.85.mlp_a_ref.refs_6_, bf16[1024,768]{1,0:T(8,128)(2,1)} %collective-permute-done.13.mlp_b_ref.refs_7_, f32[768]{0:T(1024)} %refs_8_.1), custom_call_target="tpu_custom_call" | custom-call | flops 3000000000 | bytes 9000000 | tf_op jit(solution)/shard_map/pallas_call | solution.py:668
  164.8 1.0 fusion
  165.8 1.5 collective-permute-start.26
  167.4 5.2 %collective-permute-done.27 = bf16[4,96,768]{2,1,0:T(8,128)(2,1)} collective-permute-done((bf16[4,96,768]{2,1,0:T(8,128)(2,1)}, bf16[4,96,768]{2,1,0:T(8,128)(2,1)}, u32[]{:S(2)}, u32[]{:S(2)}) %collective-permute-start.27) | collective-permute-done | bytes 589856 | tf_op jit(solution)/shard_map/ppermute | solution.py:516
  172.6 1.5 collective-permute-start.29
  174.1 1.2 add_convert_fusion.1
  175.8 1.5 collective-permute-start.28
  177.3 1.3 bitcast_add_fusion.1
  178.6 0.8 fusion.3
  179.4 13.3 %collective-permute-done.14.near_ref = bf16[512,768]{1,0:T(8,128)(2,1)} collective-permute-done((bf16[512,768]{1,0:T(8,128)(2,1)}, bf16[512,768]{1,0:T(8,128)(2,1)}, u32[]{:S(2)}, u32[]{:S(2)}) %collective-permute-start.14) | collective-permute-done | bytes 786464 | tf_op jit(solution)/shard_map/ppermute | solution.py:516
  192.7 1.6 collective-permute-start.33
  194.3 7.6 %shard_map.260 = (f32[2048,768]{1,0:T(8,128)}, bf16[512,768]{1,0:T(8,128)(2,1)}, f32[8,768]{1,0:T(8,128)}, f32[8,768]{1,0:T(8,128)}) custom-call(s32[7]{0:T(128)} %stack.100.refs_0_.info_ref, bf16[2048,768]{1,0:T(8,128)(2,1)} %x_ref.1, bf16[1024,768]{1,0:T(8,128)(2,1)} %get-tuple-element.102.grad_a_ref, ...), custom_call_target="tpu_custom_call" | custom-call | flops 7000000000 | bytes 21000000 | tf_op jit(solution)/shard_map/pallas_call | solution.py:731
  201.9 3.4 %collective-permute-done.26 = bf16[2,192,768]{2,1,0:T(8,128)(2,1)} collective-permute-done((bf16[2,192,768]{2,1,0:T(8,128)(2,1)}, bf16[2,192,768]{2,1,0:T(8,128)(2,1)}, u32[]{:S(2)}, u32[]{:S(2)}) %collective-permute-start.26) | collective-permute-done | bytes 589856 | tf_op jit(solution)/shard_map/ppermute | solution.py:516
  205.3 1.5 collective-permute-start.18
  206.8 0.8 copy-done.9
  207.7 10.3 %collective-permute-done.28 = bf16[4,96,768]{2,1,0:T(8,128)(2,1)} collective-permute-done((bf16[4,96,768]{2,1,0:T(8,128)(2,1)S(1)}, bf16[4,96,768]{2,1,0:T(8,128)(2,1)}, u32[]{:S(2)}, u32[]{:S(2)}) %collective-permute-start.28) | collective-permute-done | bytes 589856 | tf_op jit(solution)/shard_map/ppermute | solution.py:516
  218.0 1.4 bitcast_add_fusion
  219.4 0.8 fusion.4
  220.7 1.5 collective-permute-start.20
  222.2 1.0 bitcast_add_fusion.3
  223.9 10.4 %collective-permute-done.20 = f32[8,768]{1,0:T(8,128)S(1)} collective-permute-done((f32[8,768]{1,0:T(8,128)S(1)}, f32[8,768]{1,0:T(8,128)S(1)}, u32[]{:S(2)}, u32[]{:S(2)}) %collective-permute-start.20) | collective-permute-done | bytes 24608 | tf_op jit(solution)/shard_map/ppermute | solution.py:516
  235.0 1.3 convert_add_fusion
  236.2 2.0 collective-permute-done.21
  238.3 1.6 collective-permute-start.22
  240.4 2.0 collective-permute-done.22
  242.4 4.5 %shard_map.261 = bf16[2048,768]{1,0:T(8,128)(2,1)} custom-call(s32[7]{0:T(128)} %stack.100.refs_0_.info_ref, bf16[512,768]{1,0:T(8,128)(2,1)} %collective-permute-done.14.near_ref, bf16[512,768]{1,0:T(8,128)(2,1)} %collective-permute-done.15.far_ref, bf16[2048,768]{1,0:T(8,128)(2,1)} %get-tuple-element.112.whole_ref), custom_call_target="tpu_custom_call", output_to_operand_aliasing={{}: (3, {})} | custom-call | flops 3000000000 | bytes 9000000 | tf_op jit(solution)/shard_map/pallas_call | solution.py:758
  250.1 1.4 reshape.324
  252.1 1.3 fusion.10
  253.4 1.7 bitcast_add_fusion.6
  255.2 2.7 collective-permute-start.31
  257.8 1.0 bitcast_add_fusion.2
  259.3 3.6 %collective-permute-done.31 = bf16[96,768]{1,0:T(8,128)(2,1)S(1)} collective-permute-done((bf16[96,768]{1,0:T(8,128)(2,1)S(1)}, bf16[96,768]{1,0:T(8,128)(2,1)S(1)}, u32[]{:S(2)}, u32[]{:S(2)}) %collective-permute-start.31) | collective-permute-done | bytes 147488 | tf_op jit(solution)/shard_map/ppermute | solution.py:516
  263.0 0.9 copy.41
  264.6 4.7 %collective-permute-done.36 = bf16[96,768]{1,0:T(8,128)(2,1)S(1)} collective-permute-done((bf16[96,768]{1,0:T(8,128)(2,1)S(1)}, bf16[96,768]{1,0:T(8,128)(2,1)S(1)}, u32[]{:S(2)}, u32[]{:S(2)}) %collective-permute-start.36) | collective-permute-done | bytes 147488 | tf_op jit(solution)/shard_map/ppermute | solution.py:516
  270.0 2.9 %shard_map.262.whole_ref = f32[2048,768]{1,0:T(8,128)} custom-call(s32[7]{0:T(128)} %stack.100.refs_0_.info_ref, bf16[512,768]{1,0:T(8,128)(2,1)} %collective-permute-done.18.come_ref, f32[2048,768]{1,0:T(8,128)} %get-tuple-element.113.whole_ref), custom_call_target="tpu_custom_call", output_to_operand_aliasing={{}: (2, {})} | custom-call | flops 2000000000 | bytes 6000000 | tf_op jit(solution)/shard_map/pallas_call | solution.py:779
  272.9 0.9 copy-done.6
  273.8 2.9 %shard_map.263 = f32[2048,768]{1,0:T(8,128)} custom-call(s32[7]{0:T(128)} %stack.100.refs_0_.info_ref, bf16[512,768]{1,0:T(8,128)(2,1)} %copy-done.6, f32[2048,768]{1,0:T(8,128)} %shard_map.262.whole_ref), custom_call_target="tpu_custom_call", output_to_operand_aliasing={{}: (2, {})} | custom-call | flops 2000000000 | bytes 6000000 | tf_op jit(solution)/shard_map/pallas_call | solution.py:779
  (114 shorter events, 16.4 us)
Async XLA Ops:
  1.6 4.6 %copy-start.13 = (f32[2,3,64]{2,0,1:T(2,128)S(1)}, f32[2,3,64]{2,0,1:T(2,128)}, u32[]{:S(2)}) copy-start(f32[2,3,64]{2,0,1:T(2,128)} %param.20) | copy-start | bytes 4612
  1.6 4.7 %copy-start.12 = (f32[6,128]{1,0:T(8,128)S(1)}, f32[6,128]{1,0:T(8,128)}, u32[]{:S(2)}) copy-start(f32[6,128]{1,0:T(8,128)} %param.26) | copy-start | bytes 9220
  1.6 12.1 %copy-start.14 = (bf16[768,3,3,64]{0,3,2,1:T(8,128)(2,1)S(1)}, bf16[768,3,3,64]{0,3,2,1:T(8,128)(2,1)}, u32[]{:S(2)}) copy-start(bf16[768,3,3,64]{0,3,2,1:T(8,128)(2,1)} %param.19) | copy-start | bytes 2654212
  1.6 12.3 %copy-start.16 = (bf16[3,64,768]{2,1,0:T(8,128)(2,1)S(1)}, bf16[3,64,768]{2,1,0:T(8,128)(2,1)}, u32[]{:S(2)}) copy-start(bf16[3,64,768]{2,1,0:T(8,128)(2,1)} %param.21) | copy-start | bytes 884740
  1.6 7.2 %collective-permute-start = (bf16[1,96,768]{2,1,0:T(8,128)(2,1)S(1)}, bf16[1,96,768]{2,1,0:T(8,128)(2,1)S(1)}, u32[]{:S(2)}, u32[]{:S(2)}) collective-permute-start(bf16[1,96,768]{2,1,0:T(8,128)(2,1)S(1)} %dynamic-slice_bitcast_fusion), channel_id=1, source_target_pairs={{0,2},{1,3},{2,0},{3,1},{4,6},{5,7},{6,4},{7,5},{8,10},{9,11},{10,... | collective-permute-start | bytes 442376 | tf_op jit(solution)/shard_map/ppermute | solution.py:516
  6.0 10.3 %collective-permute-start.2 = (bf16[1,48,768]{2,1,0:T(8,128)(2,1)S(1)}, bf16[1,48,768]{2,1,0:T(8,128)(2,1)S(1)}, u32[]{:S(2)}, u32[]{:S(2)}) collective-permute-start(bf16[1,48,768]{2,1,0:T(8,128)(2,1)S(1)} %dynamic-slice_bitcast_fusion.1), channel_id=1, source_target_pairs={{0,2},{1,3},{2,0},{3,1},{4,6},{5,7},{6,4},{7,5},{8,10},{9,11},{10,... | collective-permute-start | bytes 221192 | tf_op jit(solution)/shard_map/ppermute | solution.py:516
  8.8 12.8 %collective-permute-start.1 = (bf16[1,96,768]{2,1,0:T(8,128)(2,1)S(1)}, bf16[1,96,768]{2,1,0:T(8,128)(2,1)S(1)}, u32[]{:S(2)}, u32[]{:S(2)}) collective-permute-start(bf16[1,96,768]{2,1,0:T(8,128)(2,1)S(1)} %collective-permute-done), channel_id=1, source_target_pairs={{0,16},{4,20},{8,24},{12,28},{16,0},{20,4},{24,8},{28,12},{1,17},{... | collective-permute-start | bytes 442376 | tf_op jit(solution)/shard_map/ppermute | solution.py:516
  11.9 24.3 %collective-permute-start.7 = (f32[1,1152]{1,0:T(1,128)S(1)}, f32[1,1152]{1,0:T(1,128)S(1)}, u32[]{:S(2)}, u32[]{:S(2)}) collective-permute-start(f32[1,1152]{1,0:T(1,128)S(1)} %pad_maximum_fusion.1), channel_id=1, source_target_pairs={{0,2},{1,3},{2,0},{3,1},{4,6},{5,7},{6,4},{7,5},{8,10},{9,11},{10,... | collective-permute-start | bytes 13832 | tf_op jit(solution)/shard_map/ppermute | solution.py:516
  13.7 25.6 %collective-permute-start.4 = (bf16[576,768]{1,0:T(8,128)(2,1)S(1)}, bf16[576,768]{1,0:T(8,128)(2,1)}, u32[]{:S(2)}, u32[]{:S(2)}) collective-permute-start(bf16[576,768]{1,0:T(8,128)(2,1)S(1)} %bitcast.129), channel_id=1, source_target_pairs={{0,2},{1,3},{2,0},{3,1},{4,6},{5,7},{6,4},{7,5},{8,10},{9,11},{10,... | collective-permute-start | bytes 2654216 | tf_op jit(solution)/shard_map/ppermute | solution.py:516
  13.9 25.3 %collective-permute-start.8 = (bf16[192,768]{1,0:T(8,128)(2,1)S(1)}, bf16[192,768]{1,0:T(8,128)(2,1)S(1)}, u32[]{:S(2)}, u32[]{:S(2)}) collective-permute-start(bf16[192,768]{1,0:T(8,128)(2,1)S(1)} %bitcast.132), channel_id=1, source_target_pairs={{0,2},{1,3},{2,0},{3,1},{4,6},{5,7},{6,4},{7,5},{8,10},{9,11},{10,... | collective-permute-start | bytes 884744 | tf_op jit(solution)/shard_map/ppermute | solution.py:516
  16.4 5.3 %collective-permute-start.3 = (bf16[1,48,768]{2,1,0:T(8,128)(2,1)S(1)}, bf16[1,48,768]{2,1,0:T(8,128)(2,1)S(1)}, u32[]{:S(2)}, u32[]{:S(2)}) collective-permute-start(bf16[1,48,768]{2,1,0:T(8,128)(2,1)S(1)} %collective-permute-done.2), channel_id=1, source_target_pairs={{0,16},{4,20},{8,24},{12,28},{16,0},{20,4},{24,8},{28,12},{1,17},{... | collective-permute-start | bytes 221192 | tf_op jit(solution)/shard_map/ppermute | solution.py:516
  21.6 14.5 %collective-permute-start.6 = (bf16[2,48,768]{2,1,0:T(8,128)(2,1)S(1)}, bf16[2,48,768]{2,1,0:T(8,128)(2,1)S(1)}, u32[]{:S(2)}, u32[]{:S(2)}) collective-permute-start(bf16[2,48,768]{2,1,0:T(8,128)(2,1)S(1)} %maximum_select_fusion.6), channel_id=1, source_target_pairs={{0,8},{4,12},{8,0},{12,4},{16,24},{20,28},{24,16},{28,20},{1,9},{5... | collective-permute-start | bytes 442376 | tf_op jit(solution)/shard_map/ppermute | solution.py:516
  23.3 12.9 %collective-permute-start.5 = (bf16[2,96,768]{2,1,0:T(8,128)(2,1)S(1)}, bf16[2,96,768]{2,1,0:T(8,128)(2,1)S(1)}, u32[]{:S(2)}, u32[]{:S(2)}) collective-permute-start(bf16[2,96,768]{2,1,0:T(8,128)(2,1)S(1)} %maximum_select_fusion.3), channel_id=1, source_target_pairs={{0,8},{4,12},{8,0},{12,4},{16,24},{20,28},{24,16},{28,20},{1,9},{5... | collective-permute-start | bytes 884744 | tf_op jit(solution)/shard_map/ppermute | solution.py:516
  39.2 0.7 copy-start.17
  52.6 24.5 %collective-permute-start.9 = (bf16[1024,768]{1,0:T(8,128)(2,1)}, bf16[1024,768]{1,0:T(8,128)(2,1)}, u32[]{:S(2)}, u32[]{:S(2)}) collective-permute-start(bf16[1024,768]{1,0:T(8,128)(2,1)} %get-tuple-element.81.branch_a_ref), channel_id=1, source_target_pairs={{0,1},{1,0},{2,3},{3,2},{4,5},{5,4},{6,7},{7,6},{8,9},{9,8},{10,11... | collective-permute-start | bytes 4718600 | tf_op jit(solution)/shard_map/ppermute | solution.py:516
  52.6 24.5 %collective-permute-start.10 = (bf16[384,768]{1,0:T(8,128)(2,1)S(1)}, bf16[384,768]{1,0:T(8,128)(2,1)S(1)}, u32[]{:S(2)}, u32[]{:S(2)}) collective-permute-start(bf16[384,768]{1,0:T(8,128)(2,1)S(1)} %get-tuple-element.150), channel_id=1, source_target_pairs={{0,2},{1,3},{2,0},{3,1},{4,6},{5,7},{6,4},{7,5},{8,10},{9,11},{10,... | collective-permute-start | bytes 1769480 | tf_op jit(solution)/shard_map/ppermute | solution.py:516
  53.3 22.7 %collective-permute-start.12 = (bf16[4,96,768]{2,1,0:T(8,128)(2,1)S(1)}, bf16[4,96,768]{2,1,0:T(8,128)(2,1)S(1)}, u32[]{:S(2)}, u32[]{:S(2)}) collective-permute-start(bf16[4,96,768]{2,1,0:T(8,128)(2,1)S(1)} %bitcast.107), channel_id=1, source_target_pairs={{0,4},{4,0},{8,12},{12,8},{16,20},{20,16},{24,28},{28,24},{1,5},{5... | collective-permute-start | bytes 1769480 | tf_op jit(solution)/shard_map/ppermute | solution.py:516
  54.9 20.2 %collective-permute-start.11 = (bf16[4,48,768]{2,1,0:T(8,128)(2,1)S(1)}, bf16[4,48,768]{2,1,0:T(8,128)(2,1)S(1)}, u32[]{:S(2)}, u32[]{:S(2)}) collective-permute-start(bf16[4,48,768]{2,1,0:T(8,128)(2,1)S(1)} %bitcast.110), channel_id=1, source_target_pairs={{0,4},{4,0},{8,12},{12,8},{16,20},{20,16},{24,28},{28,24},{1,5},{5... | collective-permute-start | bytes 884744 | tf_op jit(solution)/shard_map/ppermute | solution.py:516
  77.1 0.8 copy-start.15
  105.6 3.8 %collective-permute-start.13 = (bf16[1024,768]{1,0:T(8,128)(2,1)}, bf16[1024,768]{1,0:T(8,128)(2,1)}, u32[]{:S(2)}, u32[]{:S(2)}) collective-permute-start(bf16[1024,768]{1,0:T(8,128)(2,1)} %get-tuple-element.85.mlp_a_ref.refs_6_), channel_id=1, source_target_pairs={{0,1},{1,0},{2,3},{3,2},{4,5},{5,4},{6,7},{7,6},{8,9},{9,8},{10,11... | collective-permute-start | bytes 4718600 | tf_op jit(solution)/shard_map/ppermute | solution.py:516
  105.7 6.0 %collective-permute-start.16 = (bf16[1024,768]{1,0:T(8,128)(2,1)}, bf16[1024,768]{1,0:T(8,128)(2,1)}, u32[]{:S(2)}, u32[]{:S(2)}) collective-permute-start(bf16[1024,768]{1,0:T(8,128)(2,1)} %get-tuple-element.86.refs_1_), channel_id=1, source_target_pairs={{0,1},{1,0},{2,3},{3,2},{4,5},{5,4},{6,7},{7,6},{8,9},{9,8},{10,11... | collective-permute-start | bytes 4718600 | tf_op jit(solution)/shard_map/ppermute | solution.py:516
  106.2 51.9 %collective-permute-start.24 = (bf16[2,4,96,768]{3,2,1,0:T(8,128)(2,1)}, bf16[2,4,96,768]{3,2,1,0:T(8,128)(2,1)S(1)}, u32[]{:S(2)}, u32[]{:S(2)}) collective-permute-start(bf16[2,4,96,768]{3,2,1,0:T(8,128)(2,1)} %get-tuple-element.118), channel_id=1, source_target_pairs={{0,4},{4,0},{8,12},{12,8},{16,20},{20,16},{24,28},{28,24},{1,5},{5... | collective-permute-start | bytes 3538952 | tf_op jit(solution)/shard_map/ppermute | solution.py:516
  107.7 50.5 %collective-permute-start.25 = (bf16[2,2,192,768]{3,2,1,0:T(8,128)(2,1)}, bf16[2,2,192,768]{3,2,1,0:T(8,128)(2,1)S(1)}, u32[]{:S(2)}, u32[]{:S(2)}) collective-permute-start(bf16[2,2,192,768]{3,2,1,0:T(8,128)(2,1)} %get-tuple-element.119), channel_id=1, source_target_pairs={{0,8},{4,12},{8,0},{12,4},{16,24},{20,28},{24,16},{28,20},{1,9},{5... | collective-permute-start | bytes 3538952 | tf_op jit(solution)/shard_map/ppermute | solution.py:516
  136.8 21.4 %copy-start.2 = (bf16[2,4,96,768]{3,2,1,0:T(8,128)(2,1)S(1)}, bf16[2,4,96,768]{3,2,1,0:T(8,128)(2,1)}, u32[]{:S(2)}) copy-start(bf16[2,4,96,768]{3,2,1,0:T(8,128)(2,1)} %get-tuple-element.128) | copy-start | bytes 3538948
  156.4 37.8 %collective-permute-start.17 = (bf16[1024,768]{1,0:T(8,128)(2,1)}, bf16[1024,768]{1,0:T(8,128)(2,1)}, u32[]{:S(2)}, u32[]{:S(2)}) collective-permute-start(bf16[1024,768]{1,0:T(8,128)(2,1)} %get-tuple-element.102.grad_a_ref), channel_id=1, source_target_pairs={{0,1},{1,0},{2,3},{3,2},{4,5},{5,4},{6,7},{7,6},{8,9},{9,8},{10,11... | collective-permute-start | bytes 4718600 | tf_op jit(solution)/shard_map/ppermute | solution.py:516
  156.6 15.9 %collective-permute-start.27 = (bf16[4,96,768]{2,1,0:T(8,128)(2,1)}, bf16[4,96,768]{2,1,0:T(8,128)(2,1)}, u32[]{:S(2)}, u32[]{:S(2)}) collective-permute-start(bf16[4,96,768]{2,1,0:T(8,128)(2,1)} %get-tuple-element.122), channel_id=1, source_target_pairs={{0,4},{4,0},{8,12},{12,8},{16,20},{20,16},{24,28},{28,24},{1,5},{5... | collective-permute-start | bytes 1769480 | tf_op jit(solution)/shard_map/ppermute | solution.py:516
  158.2 6.1 %copy-start.4 = (bf16[2,4,96,768]{3,2,1,0:T(8,128)(2,1)}, bf16[2,4,96,768]{3,2,1,0:T(8,128)(2,1)S(1)}, u32[]{:S(2)}) copy-start(bf16[2,4,96,768]{3,2,1,0:T(8,128)(2,1)S(1)} %collective-permute-done.24) | copy-start | bytes 3538948
  158.2 6.7 %copy-start.1 = (bf16[2,2,192,768]{3,2,1,0:T(8,128)(2,1)}, bf16[2,2,192,768]{3,2,1,0:T(8,128)(2,1)S(1)}, u32[]{:S(2)}) copy-start(bf16[2,2,192,768]{3,2,1,0:T(8,128)(2,1)S(1)} %collective-permute-done.25) | copy-start | bytes 3538948
  159.3 5.5 %copy-start = (bf16[2,2,192,768]{3,2,1,0:T(8,128)(2,1)S(1)}, bf16[2,2,192,768]{3,2,1,0:T(8,128)(2,1)}, u32[]{:S(2)}) copy-start(bf16[2,2,192,768]{3,2,1,0:T(8,128)(2,1)} %get-tuple-element.117) | copy-start | bytes 3538948
  159.3 16.5 %collective-permute-start.32 = (bf16[4,96,768]{2,1,0:T(8,128)(2,1)}, bf16[4,96,768]{2,1,0:T(8,128)(2,1)}, u32[]{:S(2)}, u32[]{:S(2)}) collective-permute-start(bf16[4,96,768]{2,1,0:T(8,128)(2,1)} %fusion.1), channel_id=1, source_target_pairs={{0,2},{1,3},{2,0},{3,1},{4,6},{5,7},{6,4},{7,5},{8,10},{9,11},{10,... | collective-permute-start | bytes 1769480 | tf_op jit(solution)/shard_map/ppermute | solution.py:516
  164.3 9.8 %copy-start.7 = (bf16[4,96,768]{2,1,0:T(8,128)(2,1)S(1)}, bf16[4,96,768]{2,1,0:T(8,128)(2,1)}, u32[]{:S(2)}) copy-start(bf16[4,96,768]{2,1,0:T(8,128)(2,1)} %get-tuple-element.121) | copy-start | bytes 1769476
  164.3 28.4 %collective-permute-start.14 = (bf16[512,768]{1,0:T(8,128)(2,1)}, bf16[512,768]{1,0:T(8,128)(2,1)}, u32[]{:S(2)}, u32[]{:S(2)}) collective-permute-start(bf16[512,768]{1,0:T(8,128)(2,1)} %shard_map.257), channel_id=1, source_target_pairs={{0,2},{1,3},{2,0},{3,1},{4,6},{5,7},{6,4},{7,5},{8,10},{9,11},{10,... | collective-permute-start | bytes 2359304 | tf_op jit(solution)/shard_map/ppermute | solution.py:516
  164.8 12.5 %copy-start.5 = (bf16[2,4,96,768]{3,2,1,0:T(8,128)(2,1)S(1)}, bf16[2,4,96,768]{3,2,1,0:T(8,128)(2,1)}, u32[]{:S(2)}) copy-start(bf16[2,4,96,768]{3,2,1,0:T(8,128)(2,1)} %copy-done.4) | copy-start | bytes 3538948
  165.8 11.5 %copy-start.3 = (bf16[2,4,96,768]{3,2,1,0:T(8,128)(2,1)S(1)}, bf16[2,4,96,768]{3,2,1,0:T(8,128)(2,1)}, u32[]{:S(2)}) copy-start(bf16[2,4,96,768]{3,2,1,0:T(8,128)(2,1)} %get-tuple-element.128) | copy-start | bytes 3538948
  165.8 39.5 %collective-permute-start.26 = (bf16[2,192,768]{2,1,0:T(8,128)(2,1)}, bf16[2,192,768]{2,1,0:T(8,128)(2,1)}, u32[]{:S(2)}, u32[]{:S(2)}) collective-permute-start(bf16[2,192,768]{2,1,0:T(8,128)(2,1)} %fusion), channel_id=1, source_target_pairs={{0,2},{1,3},{2,0},{3,1},{4,6},{5,7},{6,4},{7,5},{8,10},{9,11},{10,... | collective-permute-start | bytes 1769480 | tf_op jit(solution)/shard_map/ppermute | solution.py:516
  172.6 34.3 %collective-permute-start.29 = (bf16[4,96,768]{2,1,0:T(8,128)(2,1)}, bf16[4,96,768]{2,1,0:T(8,128)(2,1)S(1)}, u32[]{:S(2)}, u32[]{:S(2)}) collective-permute-start(bf16[4,96,768]{2,1,0:T(8,128)(2,1)} %get-tuple-element.124), channel_id=1, source_target_pairs={{0,4},{4,0},{8,12},{12,8},{16,20},{20,16},{24,28},{28,24},{1,5},{5... | collective-permute-start | bytes 1769480 | tf_op jit(solution)/shard_map/ppermute | solution.py:516
  175.8 42.1 %collective-permute-start.28 = (bf16[4,96,768]{2,1,0:T(8,128)(2,1)S(1)}, bf16[4,96,768]{2,1,0:T(8,128)(2,1)}, u32[]{:S(2)}, u32[]{:S(2)}) collective-permute-start(bf16[4,96,768]{2,1,0:T(8,128)(2,1)S(1)} %add_convert_fusion.1), channel_id=1, source_target_pairs={{0,2},{1,3},{2,0},{3,1},{4,6},{5,7},{6,4},{7,5},{8,10},{9,11},{10,... | collective-permute-start | bytes 1769480 | tf_op jit(solution)/shard_map/ppermute | solution.py:516
  192.7 28.0 %collective-permute-start.33 = (bf16[2,96,768]{2,1,0:T(8,128)(2,1)}, bf16[2,96,768]{2,1,0:T(8,128)(2,1)}, u32[]{:S(2)}, u32[]{:S(2)}) collective-permute-start(bf16[2,96,768]{2,1,0:T(8,128)(2,1)} %fusion.3), channel_id=1, source_target_pairs={{0,8},{4,12},{8,0},{12,4},{16,24},{20,28},{24,16},{28,20},{1,9},{5... | collective-permute-start | bytes 884744 | tf_op jit(solution)/shard_map/ppermute | solution.py:516
  194.3 45.6 %collective-permute-start.15 = (bf16[512,768]{1,0:T(8,128)(2,1)}, bf16[512,768]{1,0:T(8,128)(2,1)}, u32[]{:S(2)}, u32[]{:S(2)}) collective-permute-start(bf16[512,768]{1,0:T(8,128)(2,1)} %collective-permute-done.14.near_ref), channel_id=1, source_target_pairs={{0,1},{1,0},{2,3},{3,2},{4,5},{5,4},{6,7},{7,6},{8,9},{9,8},{10,11... | collective-permute-start | bytes 2359304 | tf_op jit(solution)/shard_map/ppermute | solution.py:516
  205.3 15.4 %copy-start.18 = (f32[8,768]{1,0:T(8,128)S(1)}, f32[8,768]{1,0:T(8,128)}, u32[]{:S(2)}) copy-start(f32[8,768]{1,0:T(8,128)} %get-tuple-element.115) | copy-start | bytes 73732
  205.3 52.5 %collective-permute-start.18 = (bf16[512,768]{1,0:T(8,128)(2,1)}, bf16[512,768]{1,0:T(8,128)(2,1)}, u32[]{:S(2)}, u32[]{:S(2)}) collective-permute-start(bf16[512,768]{1,0:T(8,128)(2,1)} %get-tuple-element.109), channel_id=1, source_target_pairs={{0,2},{1,3},{2,0},{3,1},{4,6},{5,7},{6,4},{7,5},{8,10},{9,11},{10,... | collective-permute-start | bytes 2359304 | tf_op jit(solution)/shard_map/ppermute | solution.py:516
  206.8 0.8 copy-start.9
  219.4 15.0 %copy-start.11 = (f32[8,768]{1,0:T(8,128)S(1)}, f32[8,768]{1,0:T(8,128)}, u32[]{:S(2)}) copy-start(f32[8,768]{1,0:T(8,128)} %get-tuple-element.114) | copy-start | bytes 73732
  219.4 15.6 %copy-start.8 = (bf16[4,96,768]{2,1,0:T(8,128)(2,1)S(1)}, bf16[4,96,768]{2,1,0:T(8,128)(2,1)}, u32[]{:S(2)}) copy-start(bf16[4,96,768]{2,1,0:T(8,128)(2,1)} %get-tuple-element.116) | copy-start | bytes 1769476
  219.4 15.5 %copy-start.10 = (bf16[4,96,768]{2,1,0:T(8,128)(2,1)S(1)}, bf16[4,96,768]{2,1,0:T(8,128)(2,1)}, u32[]{:S(2)}) copy-start(bf16[4,96,768]{2,1,0:T(8,128)(2,1)} %copy-done.9) | copy-start | bytes 1769476
  220.2 34.9 %collective-permute-start.35 = (bf16[2,96,768]{2,1,0:T(8,128)(2,1)}, bf16[2,96,768]{2,1,0:T(8,128)(2,1)}, u32[]{:S(2)}, u32[]{:S(2)}) collective-permute-start(bf16[2,96,768]{2,1,0:T(8,128)(2,1)} %fusion.4), channel_id=1, source_target_pairs={{0,4},{4,0},{8,12},{12,8},{16,20},{20,16},{24,28},{28,24},{1,5},{5... | collective-permute-start | bytes 884744 | tf_op jit(solution)/shard_map/ppermute | solution.py:516
  220.7 13.6 %collective-permute-start.20 = (f32[8,768]{1,0:T(8,128)S(1)}, f32[8,768]{1,0:T(8,128)S(1)}, u32[]{:S(2)}, u32[]{:S(2)}) collective-permute-start(f32[8,768]{1,0:T(8,128)S(1)} %copy-done.18), channel_id=1, source_target_pairs={{0,2},{1,3},{2,0},{3,1},{4,6},{5,7},{6,4},{7,5},{8,10},{9,11},{10,... | collective-permute-start | bytes 73736 | tf_op jit(solution)/shard_map/ppermute | solution.py:516
  223.9 29.5 %collective-permute-start.34 = (bf16[96,768]{1,0:T(8,128)(2,1)}, bf16[96,768]{1,0:T(8,128)(2,1)}, u32[]{:S(2)}, u32[]{:S(2)}) collective-permute-start(bf16[96,768]{1,0:T(8,128)(2,1)} %fusion.8), channel_id=1, source_target_pairs={{0,16},{4,20},{8,24},{12,28},{16,0},{20,4},{24,8},{28,12},{1,17},{... | collective-permute-start | bytes 442376 | tf_op jit(solution)/shard_map/ppermute | solution.py:516
  234.4 3.9 %collective-permute-start.21 = (f32[8,768]{1,0:T(8,128)S(1)}, f32[8,768]{1,0:T(8,128)S(1)}, u32[]{:S(2)}, u32[]{:S(2)}) collective-permute-start(f32[8,768]{1,0:T(8,128)S(1)} %add.118), channel_id=1, source_target_pairs={{0,4},{4,0},{8,12},{12,8},{16,20},{20,16},{24,28},{28,24},{1,5},{5... | collective-permute-start | bytes 73736 | tf_op jit(solution)/shard_map/ppermute | solution.py:516
  238.3 4.1 %collective-permute-start.22 = (f32[8,768]{1,0:T(8,128)S(1)}, f32[8,768]{1,0:T(8,128)S(1)}, u32[]{:S(2)}, u32[]{:S(2)}) collective-permute-start(f32[8,768]{1,0:T(8,128)S(1)} %add.119), channel_id=1, source_target_pairs={{0,8},{4,12},{8,0},{12,4},{16,24},{20,28},{24,16},{28,20},{1,9},{5... | collective-permute-start | bytes 73736 | tf_op jit(solution)/shard_map/ppermute | solution.py:516
  239.9 15.2 %collective-permute-start.30 = (bf16[2,96,768]{2,1,0:T(8,128)(2,1)S(1)}, bf16[2,96,768]{2,1,0:T(8,128)(2,1)S(1)}, u32[]{:S(2)}, u32[]{:S(2)}) collective-permute-start(bf16[2,96,768]{2,1,0:T(8,128)(2,1)S(1)} %fusion.2), channel_id=1, source_target_pairs={{0,8},{4,12},{8,0},{12,4},{16,24},{20,28},{24,16},{28,20},{1,9},{5... | collective-permute-start | bytes 884744 | tf_op jit(solution)/shard_map/ppermute | solution.py:516
  242.4 4.8 %collective-permute-start.23 = (f32[8,768]{1,0:T(8,128)S(1)}, f32[8,768]{1,0:T(8,128)S(1)}, u32[]{:S(2)}, u32[]{:S(2)}) collective-permute-start(f32[8,768]{1,0:T(8,128)S(1)} %add.120), channel_id=1, source_target_pairs={{0,16},{4,20},{8,24},{12,28},{16,0},{20,4},{24,8},{28,12},{1,17},{... | collective-permute-start | bytes 73736 | tf_op jit(solution)/shard_map/ppermute | solution.py:516
  255.2 7.7 %collective-permute-start.31 = (bf16[96,768]{1,0:T(8,128)(2,1)S(1)}, bf16[96,768]{1,0:T(8,128)(2,1)S(1)}, u32[]{:S(2)}, u32[]{:S(2)}) collective-permute-start(bf16[96,768]{1,0:T(8,128)(2,1)S(1)} %fusion.7), channel_id=1, source_target_pairs={{0,16},{4,20},{8,24},{12,28},{16,0},{20,4},{24,8},{28,12},{1,17},{... | collective-permute-start | bytes 442376 | tf_op jit(solution)/shard_map/ppermute | solution.py:516
  257.8 15.0 %collective-permute-start.19 = (bf16[512,768]{1,0:T(8,128)(2,1)}, bf16[512,768]{1,0:T(8,128)(2,1)S(1)}, u32[]{:S(2)}, u32[]{:S(2)}) collective-permute-start(bf16[512,768]{1,0:T(8,128)(2,1)} %collective-permute-done.18.come_ref), channel_id=1, source_target_pairs={{0,1},{1,0},{2,3},{3,2},{4,5},{5,4},{6,7},{7,6},{8,9},{9,8},{10,11... | collective-permute-start | bytes 2359304 | tf_op jit(solution)/shard_map/ppermute | solution.py:516
  258.9 10.4 %collective-permute-start.36 = (bf16[96,768]{1,0:T(8,128)(2,1)S(1)}, bf16[96,768]{1,0:T(8,128)(2,1)S(1)}, u32[]{:S(2)}, u32[]{:S(2)}) collective-permute-start(bf16[96,768]{1,0:T(8,128)(2,1)S(1)} %fusion.9), channel_id=1, source_target_pairs={{0,16},{4,20},{8,24},{12,28},{16,0},{20,4},{24,8},{28,12},{1,17},{... | collective-permute-start | bytes 442376 | tf_op jit(solution)/shard_map/ppermute | solution.py:516
  272.9 0.9 copy-start.6
